TPU v7x, 512 devices: a whole 4x8x8 slice. The times are simulated.
512 devices in a mesh: ctx: 64 (over z_lo, y, core), tp: 8 (over z_hi, x).
Axes of the slice: x: 4, y: 8, z: 8 (z_hi: 2, z_lo: 4; z = z_hi * 4 + z_lo), core: 2. Of those that a mesh axis runs over, the one named last changes fastest.
Arguments:
- hidden_in: bfloat16 [16384, 2048], P('ctx', 'tp'), may hold values from -6 to 6
- ln_gain: float32 [2048], replicated, may hold values from 0.1 to 1.9
- ln_bias: float32 [2048], replicated, may hold values from -3 to 3
- w_qkv: bfloat16 [3, 2048, 2048], P(None, None, 'tp')
- w_out: bfloat16 [2048, 2048], P('tp'), may hold values from -0.375 to 0.375
- segment_ids: int32 [16384], P('ctx'), may hold values from 0 to 2, as said below
- prompt_lengths: int32 [3], replicated, may hold values from 1 to 8192, as said below
- page_table: int32 [3, 64], replicated, may hold values from -1 to 319, as said below
Outputs:
- attn_out: bfloat16 [16384, 2048], P('ctx', 'tp')
- kv_cache: bfloat16 [320, 128, 2, 2048], P('ctx', None, None, 'tp')
Inputs may be any that keep to these rules, and one draw needn't show every extreme that they name: `segment_ids`: each prompt's tokens are consecutive and the numbers never fall along the tokens; prompt i holds exactly prompt_lengths[i] tokens. `prompt_lengths`: the lengths sum to 16384; prompt 0 is shorter than 256 tokens and not a multiple of 128; prompt 1 is the longest, exactly 8192 tokens. `page_table`: for page j of prompt i with j * 128 below prompt_lengths[i], the entry is owner * 5 + slot with slot below 5, where owner is the ctx index whose tokens include the page's first token, starts_i + j * 128; distinct pages have distinct entries; all other entries are -1.
All inputs are finite; a program needn't handle non-finite values.
Results may differ from a plain program's by a relative error of at most 0.013.
Values may be sent and summed in bfloat16 or wider, within the bound.
A program may use at most 128 MiB of HBM per device.

v0:
```python
import math

import jax
import jax.numpy as jnp
from jax import lax
from jax.sharding import PartitionSpec as P

HD = 256
PAGE = 128


EPSILON = 1e-05


def passed_along(value, axis, steps):
    count = lax.axis_size(axis)
    first, last = (max(0, -steps), min(count, count - steps))
    return lax.ppermute(value, axis, [(source, source + steps) for source in range(first, last)])


def normalize(inputs, norm_gain, norm_bias):
    average = jnp.sum(inputs, axis=-1, keepdims=True) / inputs.shape[-1]
    centered = inputs - average
    spread = jnp.sum(centered * centered, axis=-1, keepdims=True) / inputs.shape[-1]
    return centered * lax.rsqrt(spread + EPSILON) * norm_gain + norm_bias


def rotary(inputs, positions):
    quarter = inputs.shape[-1] // 4
    halfway = quarter // 2
    exponent = jnp.arange(0, quarter, 2).astype(jnp.float32) / quarter
    inverse = jnp.power(jnp.float32(10000.0), -exponent)
    angles = positions.astype(jnp.float32)[:, None] * inverse[None, :]
    cosine_table = jnp.concatenate([jnp.cos(angles), jnp.cos(angles)], axis=-1)[:, None, :]
    sine_table = jnp.concatenate([jnp.sin(angles), jnp.sin(angles)], axis=-1)[:, None, :]
    leading = inputs[..., :quarter]
    turned = jnp.concatenate([-leading[..., halfway:], leading[..., :halfway]], axis=-1)
    return jnp.concatenate(
        [leading * cosine_table + turned * sine_table, inputs[..., quarter:]], axis=-1
    )


def segment_positions(segment_rows, row_index, starts):
    table_span = starts.shape[0]
    matches = segment_rows[:, None] == jnp.arange(table_span, dtype=jnp.int32)[None, :]
    first_rows = jnp.sum(jnp.where(matches, starts[None, :], 0), axis=1)
    return row_index - first_rows


def attend(carry_state, query_heads, pair_block, key_marks, query_marks, causal):
    running_max, running_sum, running_acc = carry_state
    scores = jnp.einsum(
        "qhd,khd->hqk", query_heads, pair_block[:, 0], preferred_element_type=jnp.float32
    ) / math.sqrt(query_heads.shape[-1])
    visible = query_marks[:, None] == key_marks[None, :]
    if causal:
        row_count = query_heads.shape[0]
        visible = visible & (jnp.arange(row_count)[None, :] <= jnp.arange(row_count)[:, None])
    scores = jnp.where(visible[None], scores, -jnp.inf)
    newest_max = jnp.maximum(running_max, jnp.max(scores, axis=-1))
    rescale = jnp.exp(running_max - newest_max)
    weights = jnp.exp(scores - newest_max[..., None]).astype(jnp.bfloat16)
    weights = lax.optimization_barrier(weights)
    running_sum = running_sum * rescale + jnp.sum(weights.astype(jnp.float32), axis=-1)
    running_acc = running_acc * rescale[..., None] + jnp.einsum(
        "hqk,khd->hqd", weights, pair_block[:, 1], preferred_element_type=jnp.float32
    )
    return (newest_max, running_sum, running_acc)


def visit_block(carry_state, query_heads, query_marks, pair_block, key_marks):
    tail_mark = key_marks[key_marks.shape[0] - 1]
    relevant = tail_mark == query_marks[0]
    return lax.cond(
        relevant,
        lambda current: attend(current, query_heads, pair_block, key_marks, query_marks, False),
        lambda current: current,
        carry_state,
    )


def per_device(hidden_in, ln_gain, ln_bias, w_qkv, w_out, segment_ids, prompt_lengths, page_table):
    token_rows = hidden_in.shape[0]
    model_width = w_out.shape[1]
    local_heads = w_out.shape[0] // HD
    my_index = lax.axis_index("ctx")
    reach = lax.axis_size("ctx") // 2
    whole_rows = lax.all_gather(hidden_in, "tp", axis=1, tiled=True)
    normed = normalize(whole_rows.astype(jnp.float32), ln_gain, ln_bias).astype(jnp.bfloat16)
    projected = jnp.einsum("td,jdh->tjh", normed, w_qkv, preferred_element_type=jnp.float32)
    starts = jnp.cumsum(prompt_lengths) - prompt_lengths
    row_index = my_index * token_rows + jnp.arange(token_rows, dtype=jnp.int32)
    positions = segment_positions(segment_ids, row_index, starts)
    query_heads = rotary(projected[:, 0].reshape(token_rows, local_heads, HD), positions).astype(
        jnp.bfloat16
    )
    key_heads = rotary(projected[:, 1].reshape(token_rows, local_heads, HD), positions).astype(
        jnp.bfloat16
    )
    value_heads = projected[:, 2].reshape(token_rows, local_heads, HD).astype(jnp.bfloat16)
    pair_block = jnp.stack([key_heads, value_heads], axis=1)
    own_marks = segment_ids + 1
    carry_state = (
        jnp.full((local_heads, token_rows), -jnp.inf, jnp.float32),
        jnp.zeros((local_heads, token_rows), jnp.float32),
        jnp.zeros((local_heads, token_rows, HD), jnp.float32),
    )
    carry_state = attend(carry_state, query_heads, pair_block, own_marks, own_marks, True)

    def relay_step(step, state):
        moving_pair, moving_marks, current = state
        moving_pair, moving_marks = passed_along((moving_pair, moving_marks), "ctx", 1)
        current = visit_block(current, query_heads, own_marks, moving_pair, moving_marks)
        return (moving_pair, moving_marks, current)

    carry_state = lax.fori_loop(0, reach, relay_step, (pair_block, own_marks, carry_state))[2]
    running_max, running_sum, running_acc = carry_state
    attended = (running_acc / running_sum[..., None]).astype(jnp.bfloat16)
    partial_value = jnp.einsum(
        "hqd,hde->qe",
        attended,
        w_out.reshape(local_heads, HD, model_width),
        preferred_element_type=jnp.float32,
    )
    attn_out = lax.psum_scatter(
        partial_value.astype(jnp.bfloat16), "tp", scatter_dimension=1, tiled=True
    )
    tail_pair, tail_marks = passed_along((pair_block[:PAGE], own_marks[:PAGE]), "ctx", -1)
    every_pair = jnp.concatenate([pair_block, tail_pair], axis=0)
    every_marks = jnp.concatenate([own_marks, tail_marks], axis=0)
    every_index = my_index * token_rows + jnp.arange(token_rows + PAGE, dtype=jnp.int32)
    every_segment = jnp.maximum(every_marks - 1, 0)
    every_position = segment_positions(every_segment, every_index, starts)
    page_number = every_position // PAGE
    page_offset = every_position % PAGE
    page_owner = (every_index - page_offset) // token_rows
    is_owned = (every_marks > 0) & (page_owner == my_index)
    page_count = page_table.shape[1]
    table_entry = jnp.take(
        page_table.reshape(-1),
        every_segment * page_count + jnp.clip(page_number, 0, page_count - 1),
    )
    kv_slots = token_rows // PAGE + 3
    target = jnp.where(is_owned, table_entry % kv_slots * PAGE + page_offset, -1)
    placing = (jnp.arange(kv_slots * PAGE, dtype=jnp.int32)[:, None] == target[None, :]).astype(
        jnp.bfloat16
    )
    flat_pair = every_pair.reshape(token_rows + PAGE, 2 * local_heads * HD)
    written = jnp.dot(placing, flat_pair, preferred_element_type=jnp.float32).astype(jnp.bfloat16)
    kv_cache = written.reshape(kv_slots, PAGE, 2, local_heads * HD)
    return (attn_out, kv_cache)


def solution(mesh):
    return jax.shard_map(
        per_device,
        mesh=mesh,
        in_specs=(P("ctx", "tp"), P(), P(), P(None, None, "tp"), P("tp", None), P("ctx"), P(), P()),
        out_specs=(P("ctx", "tp"), P("ctx", None, None, "tp")),
        check_vma=False,
    )
```

profile of v0, /device:TPU:16, one launch (start us, length us, event | category | flops | bytes accessed | tf_op | source)
XLA Modules:
  0.0 715.6 jit_solution(10139987149686012293)
XLA Ops:
  12.5 70.6 %all-gather.2.cloned.1.call-done = bf16[256,2048]{1,0:T(8,128)(2,1)} async-done(((bf16[256,256]{1,0:T(8,128)(2,1)}), bf16[256,2048]{1,0:T(8,128)(2,1)}) %all-gather.2.cloned.1.call-update) | async-done | bytes 1048592 | tf_op jit(solution)/shard_map/all_gather | solution.py:88
  95.1 450.4 %while.18 = (s32[]{:T(128)}, bf16[256,2,1,256]{3,0,2,1:T(8,128)(2,1)}, s32[256]{0:T(256)}, f32[1,256]{1,0:T(1,128)S(1)}, f32[1,256]{1,0:T(1,128)S(1)}, /*index=5...) while((s32[]{:T(128)}, bf16[256,2,1,256]{3,0,2,1:T(8,128)(2,1)}, ...), condition=%wide.region_11.12_spmd, body=%wide.region_6.11_spmd.sunk | while | flops 67764736 | bytes 3431739 | solution.py:116
  97.0 3.5 collective-permute-start.1
  105.5 3.2 conditional.2
  111.4 3.5 collective-permute-start.1
  119.9 3.2 conditional.2
  125.7 4.4 collective-permute-start.1
  134.2 3.2 conditional.2
  140.1 5.5 collective-permute-start.1
  149.1 3.2 conditional.2
  153.1 2.6 collective-permute-start
  155.6 5.5 collective-permute-start.1
  165.4 5.8 collective-permute-start
  171.2 5.5 collective-permute-start.1
  180.9 2.6 collective-permute-start
  183.5 8.8 %collective-permute-start.1 = (s32[256]{0:T(256)}, s32[256]{0:T(256)S(1)}, u32[]{:S(2)}, u32[]{:S(2)}) collective-permute-start(s32[256]{0:T(256)} %get-tuple-element.206), channel_id=1, source_target_pairs={{0,8},{8,16},{16,24},{24,32},{32,40},{40,48},{48,56},{56,64},{64,7... | collective-permute-start | bytes 3080 | tf_op jit(solution)/shard_map/while/body/eval_jaxpr/ppermute | solution.py:18
  196.5 2.6 collective-permute-start
  199.1 5.5 collective-permute-start.1
  208.8 5.7 collective-permute-start
  214.5 5.6 collective-permute-start.1
  224.3 2.6 collective-permute-start
  226.9 8.8 %collective-permute-start.1 = (s32[256]{0:T(256)}, s32[256]{0:T(256)S(1)}, u32[]{:S(2)}, u32[]{:S(2)}) collective-permute-start(s32[256]{0:T(256)} %get-tuple-element.206), channel_id=1, source_target_pairs={{0,8},{8,16},{16,24},{24,32},{32,40},{40,48},{48,56},{56,64},{64,7... | collective-permute-start | bytes 3080 | tf_op jit(solution)/shard_map/while/body/eval_jaxpr/ppermute | solution.py:18
  239.9 2.6 collective-permute-start
  242.5 5.5 collective-permute-start.1
  254.8 5.5 collective-permute-start.1
  264.5 2.6 collective-permute-start
  267.1 5.5 collective-permute-start.1
  276.9 2.6 collective-permute-start
  279.5 5.5 collective-permute-start.1
  289.2 4.4 collective-permute-start
  293.6 6.7 collective-permute-start.1
  307.1 9.7 %collective-permute-start.1 = (s32[256]{0:T(256)}, s32[256]{0:T(256)S(1)}, u32[]{:S(2)}, u32[]{:S(2)}) collective-permute-start(s32[256]{0:T(256)} %get-tuple-element.206), channel_id=1, source_target_pairs={{0,8},{8,16},{16,24},{24,32},{32,40},{40,48},{48,56},{56,64},{64,7... | collective-permute-start | bytes 3080 | tf_op jit(solution)/shard_map/while/body/eval_jaxpr/ppermute | solution.py:18
  323.5 6.4 collective-permute-start.1
  334.2 5.4 collective-permute-start
  339.6 6.8 collective-permute-start.1
  350.6 2.6 collective-permute-start
  353.2 9.7 %collective-permute-start.1 = (s32[256]{0:T(256)}, s32[256]{0:T(256)S(1)}, u32[]{:S(2)}, u32[]{:S(2)}) collective-permute-start(s32[256]{0:T(256)} %get-tuple-element.206), channel_id=1, source_target_pairs={{0,8},{8,16},{16,24},{24,32},{32,40},{40,48},{48,56},{56,64},{64,7... | collective-permute-start | bytes 3080 | tf_op jit(solution)/shard_map/while/body/eval_jaxpr/ppermute | solution.py:18
  367.0 2.6 collective-permute-start
  369.6 6.4 collective-permute-start.1
  380.3 5.3 collective-permute-start
  385.6 6.9 collective-permute-start.1
  399.3 9.7 %collective-permute-start.1 = (s32[256]{0:T(256)}, s32[256]{0:T(256)S(1)}, u32[]{:S(2)}, u32[]{:S(2)}) collective-permute-start(s32[256]{0:T(256)} %get-tuple-element.206), channel_id=1, source_target_pairs={{0,8},{8,16},{16,24},{24,32},{32,40},{40,48},{48,56},{56,64},{64,7... | collective-permute-start | bytes 3080 | tf_op jit(solution)/shard_map/while/body/eval_jaxpr/ppermute | solution.py:18
  413.2 2.6 collective-permute-start
  415.8 6.4 collective-permute-start.1
  429.0 6.4 collective-permute-start.1
  439.6 2.6 collective-permute-start
  442.2 6.4 collective-permute-start.1
  455.4 6.4 collective-permute-start.1
  466.1 2.6 collective-permute-start
  468.7 6.4 collective-permute-start.1
  479.3 2.6 collective-permute-start
  481.9 6.4 collective-permute-start.1
  495.1 6.4 collective-permute-start.1
  505.8 2.6 collective-permute-start
  508.3 6.4 collective-permute-start.1
  521.6 6.4 collective-permute-start.1
  532.2 2.6 collective-permute-start
  534.8 6.4 collective-permute-start.1
  545.4 2.8 convolution_convert_fusion
  552.4 3.9 gather_fusion
  556.4 3.6 collective-permute-start.3
  560.7 3.6 collective-permute-done.3
  566.6 2.7 reshape.659
  569.3 139.4 %reduce-scatter.2.cloned.1.call-done = bf16[256,256]{1,0:T(8,128)(2,1)} async-done(((bf16[256,2048]{1,0:T(8,128)(2,1)}), bf16[256,256]{1,0:T(8,128)(2,1)}) %reduce-scatter.2.cloned.1.call-update) | async-done | bytes 131088 | tf_op jit(solution)/shard_map/reduce_scatter | solution.py:125
  (327 shorter events, 163.2 us)
Async XLA Ops:
  7.2 75.8 %all-gather.2.cloned.1.call-start = ((), (), s32[]{:S(2)}) async-start(), calls=%async_computation.1 | async-start | bytes 1179648 | tf_op jit(solution)/shard_map/all_gather | solution.py:88
  7.9 700.8 %reduce-scatter.2.cloned.1.call-start = ((), (), s32[]{:S(2)}) async-start(), calls=%async_computation.2 | async-start | bytes 1179648 | tf_op jit(solution)/shard_map/reduce_scatter | solution.py:125
  95.1 10.4 %collective-permute-start = (bf16[256,2,1,256]{3,0,2,1:T(8,128)(2,1)}, bf16[256,2,1,256]{3,0,2,1:T(8,128)(2,1)S(1)}, u32[]{:S(2)}, u32[]{:S(2)}) collective-permute-start(bf16[256,2,1,256]{3,0,2,1:T(8,128)(2,1)} %get-tuple-element.205), channel_id=1, source_target_pairs={{0,8},{8,16},{16,24},{24,32},{32,40},{40,48},{48,56},{56,64},{64,7... | collective-permute-start | bytes 786440 | tf_op jit(solution)/shard_map/while/body/eval_jaxpr/ppermute | solution.py:18
  109.4 10.4 %collective-permute-start = (bf16[256,2,1,256]{3,0,2,1:T(8,128)(2,1)}, bf16[256,2,1,256]{3,0,2,1:T(8,128)(2,1)S(1)}, u32[]{:S(2)}, u32[]{:S(2)}) collective-permute-start(bf16[256,2,1,256]{3,0,2,1:T(8,128)(2,1)} %get-tuple-element.205), channel_id=1, source_target_pairs={{0,8},{8,16},{16,24},{24,32},{32,40},{40,48},{48,56},{56,64},{64,7... | collective-permute-start | bytes 786440 | tf_op jit(solution)/shard_map/while/body/eval_jaxpr/ppermute | solution.py:18
  123.8 10.4 %collective-permute-start = (bf16[256,2,1,256]{3,0,2,1:T(8,128)(2,1)}, bf16[256,2,1,256]{3,0,2,1:T(8,128)(2,1)S(1)}, u32[]{:S(2)}, u32[]{:S(2)}) collective-permute-start(bf16[256,2,1,256]{3,0,2,1:T(8,128)(2,1)} %get-tuple-element.205), channel_id=1, source_target_pairs={{0,8},{8,16},{16,24},{24,32},{32,40},{40,48},{48,56},{56,64},{64,7... | collective-permute-start | bytes 786440 | tf_op jit(solution)/shard_map/while/body/eval_jaxpr/ppermute | solution.py:18
  138.1 11.0 %collective-permute-start = (bf16[256,2,1,256]{3,0,2,1:T(8,128)(2,1)}, bf16[256,2,1,256]{3,0,2,1:T(8,128)(2,1)S(1)}, u32[]{:S(2)}, u32[]{:S(2)}) collective-permute-start(bf16[256,2,1,256]{3,0,2,1:T(8,128)(2,1)} %get-tuple-element.205), channel_id=1, source_target_pairs={{0,8},{8,16},{16,24},{24,32},{32,40},{40,48},{48,56},{56,64},{64,7... | collective-permute-start | bytes 786440 | tf_op jit(solution)/shard_map/while/body/eval_jaxpr/ppermute | solution.py:18
  140.1 6.6 collective-permute-start.1
  153.1 11.6 %collective-permute-start = (bf16[256,2,1,256]{3,0,2,1:T(8,128)(2,1)}, bf16[256,2,1,256]{3,0,2,1:T(8,128)(2,1)S(1)}, u32[]{:S(2)}, u32[]{:S(2)}) collective-permute-start(bf16[256,2,1,256]{3,0,2,1:T(8,128)(2,1)} %get-tuple-element.205), channel_id=1, source_target_pairs={{0,8},{8,16},{16,24},{24,32},{32,40},{40,48},{48,56},{56,64},{64,7... | collective-permute-start | bytes 786440 | tf_op jit(solution)/shard_map/while/body/eval_jaxpr/ppermute | solution.py:18
  155.6 6.6 collective-permute-start.1
  165.4 14.8 %collective-permute-start = (bf16[256,2,1,256]{3,0,2,1:T(8,128)(2,1)}, bf16[256,2,1,256]{3,0,2,1:T(8,128)(2,1)S(1)}, u32[]{:S(2)}, u32[]{:S(2)}) collective-permute-start(bf16[256,2,1,256]{3,0,2,1:T(8,128)(2,1)} %get-tuple-element.205), channel_id=1, source_target_pairs={{0,8},{8,16},{16,24},{24,32},{32,40},{40,48},{48,56},{56,64},{64,7... | collective-permute-start | bytes 786440 | tf_op jit(solution)/shard_map/while/body/eval_jaxpr/ppermute | solution.py:18
  171.2 6.6 collective-permute-start.1
  180.9 14.8 %collective-permute-start = (bf16[256,2,1,256]{3,0,2,1:T(8,128)(2,1)}, bf16[256,2,1,256]{3,0,2,1:T(8,128)(2,1)S(1)}, u32[]{:S(2)}, u32[]{:S(2)}) collective-permute-start(bf16[256,2,1,256]{3,0,2,1:T(8,128)(2,1)} %get-tuple-element.205), channel_id=1, source_target_pairs={{0,8},{8,16},{16,24},{24,32},{32,40},{40,48},{48,56},{56,64},{64,7... | collective-permute-start | bytes 786440 | tf_op jit(solution)/shard_map/while/body/eval_jaxpr/ppermute | solution.py:18
  183.5 9.8 %collective-permute-start.1 = (s32[256]{0:T(256)}, s32[256]{0:T(256)S(1)}, u32[]{:S(2)}, u32[]{:S(2)}) collective-permute-start(s32[256]{0:T(256)} %get-tuple-element.206), channel_id=1, source_target_pairs={{0,8},{8,16},{16,24},{24,32},{32,40},{40,48},{48,56},{56,64},{64,7... | collective-permute-start | bytes 3080 | tf_op jit(solution)/shard_map/while/body/eval_jaxpr/ppermute | solution.py:18
  196.5 11.6 %collective-permute-start = (bf16[256,2,1,256]{3,0,2,1:T(8,128)(2,1)}, bf16[256,2,1,256]{3,0,2,1:T(8,128)(2,1)S(1)}, u32[]{:S(2)}, u32[]{:S(2)}) collective-permute-start(bf16[256,2,1,256]{3,0,2,1:T(8,128)(2,1)} %get-tuple-element.205), channel_id=1, source_target_pairs={{0,8},{8,16},{16,24},{24,32},{32,40},{40,48},{48,56},{56,64},{64,7... | collective-permute-start | bytes 786440 | tf_op jit(solution)/shard_map/while/body/eval_jaxpr/ppermute | solution.py:18
  199.1 6.6 collective-permute-start.1
  208.8 14.8 %collective-permute-start = (bf16[256,2,1,256]{3,0,2,1:T(8,128)(2,1)}, bf16[256,2,1,256]{3,0,2,1:T(8,128)(2,1)S(1)}, u32[]{:S(2)}, u32[]{:S(2)}) collective-permute-start(bf16[256,2,1,256]{3,0,2,1:T(8,128)(2,1)} %get-tuple-element.205), channel_id=1, source_target_pairs={{0,8},{8,16},{16,24},{24,32},{32,40},{40,48},{48,56},{56,64},{64,7... | collective-permute-start | bytes 786440 | tf_op jit(solution)/shard_map/while/body/eval_jaxpr/ppermute | solution.py:18
  214.5 6.7 collective-permute-start.1
  224.3 14.8 %collective-permute-start = (bf16[256,2,1,256]{3,0,2,1:T(8,128)(2,1)}, bf16[256,2,1,256]{3,0,2,1:T(8,128)(2,1)S(1)}, u32[]{:S(2)}, u32[]{:S(2)}) collective-permute-start(bf16[256,2,1,256]{3,0,2,1:T(8,128)(2,1)} %get-tuple-element.205), channel_id=1, source_target_pairs={{0,8},{8,16},{16,24},{24,32},{32,40},{40,48},{48,56},{56,64},{64,7... | collective-permute-start | bytes 786440 | tf_op jit(solution)/shard_map/while/body/eval_jaxpr/ppermute | solution.py:18
  226.9 9.8 %collective-permute-start.1 = (s32[256]{0:T(256)}, s32[256]{0:T(256)S(1)}, u32[]{:S(2)}, u32[]{:S(2)}) collective-permute-start(s32[256]{0:T(256)} %get-tuple-element.206), channel_id=1, source_target_pairs={{0,8},{8,16},{16,24},{24,32},{32,40},{40,48},{48,56},{56,64},{64,7... | collective-permute-start | bytes 3080 | tf_op jit(solution)/shard_map/while/body/eval_jaxpr/ppermute | solution.py:18
  239.9 11.6 %collective-permute-start = (bf16[256,2,1,256]{3,0,2,1:T(8,128)(2,1)}, bf16[256,2,1,256]{3,0,2,1:T(8,128)(2,1)S(1)}, u32[]{:S(2)}, u32[]{:S(2)}) collective-permute-start(bf16[256,2,1,256]{3,0,2,1:T(8,128)(2,1)} %get-tuple-element.205), channel_id=1, source_target_pairs={{0,8},{8,16},{16,24},{24,32},{32,40},{40,48},{48,56},{56,64},{64,7... | collective-permute-start | bytes 786440 | tf_op jit(solution)/shard_map/while/body/eval_jaxpr/ppermute | solution.py:18
  242.5 6.6 collective-permute-start.1
  252.2 11.6 %collective-permute-start = (bf16[256,2,1,256]{3,0,2,1:T(8,128)(2,1)}, bf16[256,2,1,256]{3,0,2,1:T(8,128)(2,1)S(1)}, u32[]{:S(2)}, u32[]{:S(2)}) collective-permute-start(bf16[256,2,1,256]{3,0,2,1:T(8,128)(2,1)} %get-tuple-element.205), channel_id=1, source_target_pairs={{0,8},{8,16},{16,24},{24,32},{32,40},{40,48},{48,56},{56,64},{64,7... | collective-permute-start | bytes 786440 | tf_op jit(solution)/shard_map/while/body/eval_jaxpr/ppermute | solution.py:18
  254.8 6.6 collective-permute-start.1
  264.5 11.6 %collective-permute-start = (bf16[256,2,1,256]{3,0,2,1:T(8,128)(2,1)}, bf16[256,2,1,256]{3,0,2,1:T(8,128)(2,1)S(1)}, u32[]{:S(2)}, u32[]{:S(2)}) collective-permute-start(bf16[256,2,1,256]{3,0,2,1:T(8,128)(2,1)} %get-tuple-element.205), channel_id=1, source_target_pairs={{0,8},{8,16},{16,24},{24,32},{32,40},{40,48},{48,56},{56,64},{64,7... | collective-permute-start | bytes 786440 | tf_op jit(solution)/shard_map/while/body/eval_jaxpr/ppermute | solution.py:18
  267.1 6.6 collective-permute-start.1
  276.9 11.6 %collective-permute-start = (bf16[256,2,1,256]{3,0,2,1:T(8,128)(2,1)}, bf16[256,2,1,256]{3,0,2,1:T(8,128)(2,1)S(1)}, u32[]{:S(2)}, u32[]{:S(2)}) collective-permute-start(bf16[256,2,1,256]{3,0,2,1:T(8,128)(2,1)} %get-tuple-element.205), channel_id=1, source_target_pairs={{0,8},{8,16},{16,24},{24,32},{32,40},{40,48},{48,56},{56,64},{64,7... | collective-permute-start | bytes 786440 | tf_op jit(solution)/shard_map/while/body/eval_jaxpr/ppermute | solution.py:18
  279.5 6.6 collective-permute-start.1
  289.2 14.6 %collective-permute-start = (bf16[256,2,1,256]{3,0,2,1:T(8,128)(2,1)}, bf16[256,2,1,256]{3,0,2,1:T(8,128)(2,1)S(1)}, u32[]{:S(2)}, u32[]{:S(2)}) collective-permute-start(bf16[256,2,1,256]{3,0,2,1:T(8,128)(2,1)} %get-tuple-element.205), channel_id=1, source_target_pairs={{0,8},{8,16},{16,24},{24,32},{32,40},{40,48},{48,56},{56,64},{64,7... | collective-permute-start | bytes 786440 | tf_op jit(solution)/shard_map/while/body/eval_jaxpr/ppermute | solution.py:18
  293.6 7.7 %collective-permute-start.1 = (s32[256]{0:T(256)}, s32[256]{0:T(256)S(1)}, u32[]{:S(2)}, u32[]{:S(2)}) collective-permute-start(s32[256]{0:T(256)} %get-tuple-element.206), channel_id=1, source_target_pairs={{0,8},{8,16},{16,24},{24,32},{32,40},{40,48},{48,56},{56,64},{64,7... | collective-permute-start | bytes 3080 | tf_op jit(solution)/shard_map/while/body/eval_jaxpr/ppermute | solution.py:18
  304.5 15.7 %collective-permute-start = (bf16[256,2,1,256]{3,0,2,1:T(8,128)(2,1)}, bf16[256,2,1,256]{3,0,2,1:T(8,128)(2,1)S(1)}, u32[]{:S(2)}, u32[]{:S(2)}) collective-permute-start(bf16[256,2,1,256]{3,0,2,1:T(8,128)(2,1)} %get-tuple-element.205), channel_id=1, source_target_pairs={{0,8},{8,16},{16,24},{24,32},{32,40},{40,48},{48,56},{56,64},{64,7... | collective-permute-start | bytes 786440 | tf_op jit(solution)/shard_map/while/body/eval_jaxpr/ppermute | solution.py:18
  307.1 10.7 %collective-permute-start.1 = (s32[256]{0:T(256)}, s32[256]{0:T(256)S(1)}, u32[]{:S(2)}, u32[]{:S(2)}) collective-permute-start(s32[256]{0:T(256)} %get-tuple-element.206), channel_id=1, source_target_pairs={{0,8},{8,16},{16,24},{24,32},{32,40},{40,48},{48,56},{56,64},{64,7... | collective-permute-start | bytes 3080 | tf_op jit(solution)/shard_map/while/body/eval_jaxpr/ppermute | solution.py:18
  320.9 12.5 %collective-permute-start = (bf16[256,2,1,256]{3,0,2,1:T(8,128)(2,1)}, bf16[256,2,1,256]{3,0,2,1:T(8,128)(2,1)S(1)}, u32[]{:S(2)}, u32[]{:S(2)}) collective-permute-start(bf16[256,2,1,256]{3,0,2,1:T(8,128)(2,1)} %get-tuple-element.205), channel_id=1, source_target_pairs={{0,8},{8,16},{16,24},{24,32},{32,40},{40,48},{48,56},{56,64},{64,7... | collective-permute-start | bytes 786440 | tf_op jit(solution)/shard_map/while/body/eval_jaxpr/ppermute | solution.py:18
  323.5 7.5 %collective-permute-start.1 = (s32[256]{0:T(256)}, s32[256]{0:T(256)S(1)}, u32[]{:S(2)}, u32[]{:S(2)}) collective-permute-start(s32[256]{0:T(256)} %get-tuple-element.206), channel_id=1, source_target_pairs={{0,8},{8,16},{16,24},{24,32},{32,40},{40,48},{48,56},{56,64},{64,7... | collective-permute-start | bytes 3080 | tf_op jit(solution)/shard_map/while/body/eval_jaxpr/ppermute | solution.py:18
  334.2 15.7 %collective-permute-start = (bf16[256,2,1,256]{3,0,2,1:T(8,128)(2,1)}, bf16[256,2,1,256]{3,0,2,1:T(8,128)(2,1)S(1)}, u32[]{:S(2)}, u32[]{:S(2)}) collective-permute-start(bf16[256,2,1,256]{3,0,2,1:T(8,128)(2,1)} %get-tuple-element.205), channel_id=1, source_target_pairs={{0,8},{8,16},{16,24},{24,32},{32,40},{40,48},{48,56},{56,64},{64,7... | collective-permute-start | bytes 786440 | tf_op jit(solution)/shard_map/while/body/eval_jaxpr/ppermute | solution.py:18
  339.6 7.8 %collective-permute-start.1 = (s32[256]{0:T(256)}, s32[256]{0:T(256)S(1)}, u32[]{:S(2)}, u32[]{:S(2)}) collective-permute-start(s32[256]{0:T(256)} %get-tuple-element.206), channel_id=1, source_target_pairs={{0,8},{8,16},{16,24},{24,32},{32,40},{40,48},{48,56},{56,64},{64,7... | collective-permute-start | bytes 3080 | tf_op jit(solution)/shard_map/while/body/eval_jaxpr/ppermute | solution.py:18
  350.6 15.7 %collective-permute-start = (bf16[256,2,1,256]{3,0,2,1:T(8,128)(2,1)}, bf16[256,2,1,256]{3,0,2,1:T(8,128)(2,1)S(1)}, u32[]{:S(2)}, u32[]{:S(2)}) collective-permute-start(bf16[256,2,1,256]{3,0,2,1:T(8,128)(2,1)} %get-tuple-element.205), channel_id=1, source_target_pairs={{0,8},{8,16},{16,24},{24,32},{32,40},{40,48},{48,56},{56,64},{64,7... | collective-permute-start | bytes 786440 | tf_op jit(solution)/shard_map/while/body/eval_jaxpr/ppermute | solution.py:18
  353.2 10.7 %collective-permute-start.1 = (s32[256]{0:T(256)}, s32[256]{0:T(256)S(1)}, u32[]{:S(2)}, u32[]{:S(2)}) collective-permute-start(s32[256]{0:T(256)} %get-tuple-element.206), channel_id=1, source_target_pairs={{0,8},{8,16},{16,24},{24,32},{32,40},{40,48},{48,56},{56,64},{64,7... | collective-permute-start | bytes 3080 | tf_op jit(solution)/shard_map/while/body/eval_jaxpr/ppermute | solution.py:18
  367.0 12.5 %collective-permute-start = (bf16[256,2,1,256]{3,0,2,1:T(8,128)(2,1)}, bf16[256,2,1,256]{3,0,2,1:T(8,128)(2,1)S(1)}, u32[]{:S(2)}, u32[]{:S(2)}) collective-permute-start(bf16[256,2,1,256]{3,0,2,1:T(8,128)(2,1)} %get-tuple-element.205), channel_id=1, source_target_pairs={{0,8},{8,16},{16,24},{24,32},{32,40},{40,48},{48,56},{56,64},{64,7... | collective-permute-start | bytes 786440 | tf_op jit(solution)/shard_map/while/body/eval_jaxpr/ppermute | solution.py:18
  369.6 7.5 %collective-permute-start.1 = (s32[256]{0:T(256)}, s32[256]{0:T(256)S(1)}, u32[]{:S(2)}, u32[]{:S(2)}) collective-permute-start(s32[256]{0:T(256)} %get-tuple-element.206), channel_id=1, source_target_pairs={{0,8},{8,16},{16,24},{24,32},{32,40},{40,48},{48,56},{56,64},{64,7... | collective-permute-start | bytes 3080 | tf_op jit(solution)/shard_map/while/body/eval_jaxpr/ppermute | solution.py:18
  380.3 15.7 %collective-permute-start = (bf16[256,2,1,256]{3,0,2,1:T(8,128)(2,1)}, bf16[256,2,1,256]{3,0,2,1:T(8,128)(2,1)S(1)}, u32[]{:S(2)}, u32[]{:S(2)}) collective-permute-start(bf16[256,2,1,256]{3,0,2,1:T(8,128)(2,1)} %get-tuple-element.205), channel_id=1, source_target_pairs={{0,8},{8,16},{16,24},{24,32},{32,40},{40,48},{48,56},{56,64},{64,7... | collective-permute-start | bytes 786440 | tf_op jit(solution)/shard_map/while/body/eval_jaxpr/ppermute | solution.py:18
  385.6 7.9 %collective-permute-start.1 = (s32[256]{0:T(256)}, s32[256]{0:T(256)S(1)}, u32[]{:S(2)}, u32[]{:S(2)}) collective-permute-start(s32[256]{0:T(256)} %get-tuple-element.206), channel_id=1, source_target_pairs={{0,8},{8,16},{16,24},{24,32},{32,40},{40,48},{48,56},{56,64},{64,7... | collective-permute-start | bytes 3080 | tf_op jit(solution)/shard_map/while/body/eval_jaxpr/ppermute | solution.py:18
  396.7 15.7 %collective-permute-start = (bf16[256,2,1,256]{3,0,2,1:T(8,128)(2,1)}, bf16[256,2,1,256]{3,0,2,1:T(8,128)(2,1)S(1)}, u32[]{:S(2)}, u32[]{:S(2)}) collective-permute-start(bf16[256,2,1,256]{3,0,2,1:T(8,128)(2,1)} %get-tuple-element.205), channel_id=1, source_target_pairs={{0,8},{8,16},{16,24},{24,32},{32,40},{40,48},{48,56},{56,64},{64,7... | collective-permute-start | bytes 786440 | tf_op jit(solution)/shard_map/while/body/eval_jaxpr/ppermute | solution.py:18
  399.3 10.7 %collective-permute-start.1 = (s32[256]{0:T(256)}, s32[256]{0:T(256)S(1)}, u32[]{:S(2)}, u32[]{:S(2)}) collective-permute-start(s32[256]{0:T(256)} %get-tuple-element.206), channel_id=1, source_target_pairs={{0,8},{8,16},{16,24},{24,32},{32,40},{40,48},{48,56},{56,64},{64,7... | collective-permute-start | bytes 3080 | tf_op jit(solution)/shard_map/while/body/eval_jaxpr/ppermute | solution.py:18
  413.2 12.5 %collective-permute-start = (bf16[256,2,1,256]{3,0,2,1:T(8,128)(2,1)}, bf16[256,2,1,256]{3,0,2,1:T(8,128)(2,1)S(1)}, u32[]{:S(2)}, u32[]{:S(2)}) collective-permute-start(bf16[256,2,1,256]{3,0,2,1:T(8,128)(2,1)} %get-tuple-element.205), channel_id=1, source_target_pairs={{0,8},{8,16},{16,24},{24,32},{32,40},{40,48},{48,56},{56,64},{64,7... | collective-permute-start | bytes 786440 | tf_op jit(solution)/shard_map/while/body/eval_jaxpr/ppermute | solution.py:18
  415.8 7.5 %collective-permute-start.1 = (s32[256]{0:T(256)}, s32[256]{0:T(256)S(1)}, u32[]{:S(2)}, u32[]{:S(2)}) collective-permute-start(s32[256]{0:T(256)} %get-tuple-element.206), channel_id=1, source_target_pairs={{0,8},{8,16},{16,24},{24,32},{32,40},{40,48},{48,56},{56,64},{64,7... | collective-permute-start | bytes 3080 | tf_op jit(solution)/shard_map/while/body/eval_jaxpr/ppermute | solution.py:18
  426.4 12.5 %collective-permute-start = (bf16[256,2,1,256]{3,0,2,1:T(8,128)(2,1)}, bf16[256,2,1,256]{3,0,2,1:T(8,128)(2,1)S(1)}, u32[]{:S(2)}, u32[]{:S(2)}) collective-permute-start(bf16[256,2,1,256]{3,0,2,1:T(8,128)(2,1)} %get-tuple-element.205), channel_id=1, source_target_pairs={{0,8},{8,16},{16,24},{24,32},{32,40},{40,48},{48,56},{56,64},{64,7... | collective-permute-start | bytes 786440 | tf_op jit(solution)/shard_map/while/body/eval_jaxpr/ppermute | solution.py:18
  429.0 7.5 %collective-permute-start.1 = (s32[256]{0:T(256)}, s32[256]{0:T(256)S(1)}, u32[]{:S(2)}, u32[]{:S(2)}) collective-permute-start(s32[256]{0:T(256)} %get-tuple-element.206), channel_id=1, source_target_pairs={{0,8},{8,16},{16,24},{24,32},{32,40},{40,48},{48,56},{56,64},{64,7... | collective-permute-start | bytes 3080 | tf_op jit(solution)/shard_map/while/body/eval_jaxpr/ppermute | solution.py:18
  439.6 12.5 %collective-permute-start = (bf16[256,2,1,256]{3,0,2,1:T(8,128)(2,1)}, bf16[256,2,1,256]{3,0,2,1:T(8,128)(2,1)S(1)}, u32[]{:S(2)}, u32[]{:S(2)}) collective-permute-start(bf16[256,2,1,256]{3,0,2,1:T(8,128)(2,1)} %get-tuple-element.205), channel_id=1, source_target_pairs={{0,8},{8,16},{16,24},{24,32},{32,40},{40,48},{48,56},{56,64},{64,7... | collective-permute-start | bytes 786440 | tf_op jit(solution)/shard_map/while/body/eval_jaxpr/ppermute | solution.py:18
  442.2 7.5 %collective-permute-start.1 = (s32[256]{0:T(256)}, s32[256]{0:T(256)S(1)}, u32[]{:S(2)}, u32[]{:S(2)}) collective-permute-start(s32[256]{0:T(256)} %get-tuple-element.206), channel_id=1, source_target_pairs={{0,8},{8,16},{16,24},{24,32},{32,40},{40,48},{48,56},{56,64},{64,7... | collective-permute-start | bytes 3080 | tf_op jit(solution)/shard_map/while/body/eval_jaxpr/ppermute | solution.py:18
  452.8 12.5 %collective-permute-start = (bf16[256,2,1,256]{3,0,2,1:T(8,128)(2,1)}, bf16[256,2,1,256]{3,0,2,1:T(8,128)(2,1)S(1)}, u32[]{:S(2)}, u32[]{:S(2)}) collective-permute-start(bf16[256,2,1,256]{3,0,2,1:T(8,128)(2,1)} %get-tuple-element.205), channel_id=1, source_target_pairs={{0,8},{8,16},{16,24},{24,32},{32,40},{40,48},{48,56},{56,64},{64,7... | collective-permute-start | bytes 786440 | tf_op jit(solution)/shard_map/while/body/eval_jaxpr/ppermute | solution.py:18
  455.4 7.5 %collective-permute-start.1 = (s32[256]{0:T(256)}, s32[256]{0:T(256)S(1)}, u32[]{:S(2)}, u32[]{:S(2)}) collective-permute-start(s32[256]{0:T(256)} %get-tuple-element.206), channel_id=1, source_target_pairs={{0,8},{8,16},{16,24},{24,32},{32,40},{40,48},{48,56},{56,64},{64,7... | collective-permute-start | bytes 3080 | tf_op jit(solution)/shard_map/while/body/eval_jaxpr/ppermute | solution.py:18
  466.1 12.5 %collective-permute-start = (bf16[256,2,1,256]{3,0,2,1:T(8,128)(2,1)}, bf16[256,2,1,256]{3,0,2,1:T(8,128)(2,1)S(1)}, u32[]{:S(2)}, u32[]{:S(2)}) collective-permute-start(bf16[256,2,1,256]{3,0,2,1:T(8,128)(2,1)} %get-tuple-element.205), channel_id=1, source_target_pairs={{0,8},{8,16},{16,24},{24,32},{32,40},{40,48},{48,56},{56,64},{64,7... | collective-permute-start | bytes 786440 | tf_op jit(solution)/shard_map/while/body/eval_jaxpr/ppermute | solution.py:18
  468.7 7.5 %collective-permute-start.1 = (s32[256]{0:T(256)}, s32[256]{0:T(256)S(1)}, u32[]{:S(2)}, u32[]{:S(2)}) collective-permute-start(s32[256]{0:T(256)} %get-tuple-element.206), channel_id=1, source_target_pairs={{0,8},{8,16},{16,24},{24,32},{32,40},{40,48},{48,56},{56,64},{64,7... | collective-permute-start | bytes 3080 | tf_op jit(solution)/shard_map/while/body/eval_jaxpr/ppermute | solution.py:18
  479.3 12.5 %collective-permute-start = (bf16[256,2,1,256]{3,0,2,1:T(8,128)(2,1)}, bf16[256,2,1,256]{3,0,2,1:T(8,128)(2,1)S(1)}, u32[]{:S(2)}, u32[]{:S(2)}) collective-permute-start(bf16[256,2,1,256]{3,0,2,1:T(8,128)(2,1)} %get-tuple-element.205), channel_id=1, source_target_pairs={{0,8},{8,16},{16,24},{24,32},{32,40},{40,48},{48,56},{56,64},{64,7... | collective-permute-start | bytes 786440 | tf_op jit(solution)/shard_map/while/body/eval_jaxpr/ppermute | solution.py:18
  481.9 7.5 %collective-permute-start.1 = (s32[256]{0:T(256)}, s32[256]{0:T(256)S(1)}, u32[]{:S(2)}, u32[]{:S(2)}) collective-permute-start(s32[256]{0:T(256)} %get-tuple-element.206), channel_id=1, source_target_pairs={{0,8},{8,16},{16,24},{24,32},{32,40},{40,48},{48,56},{56,64},{64,7... | collective-permute-start | bytes 3080 | tf_op jit(solution)/shard_map/while/body/eval_jaxpr/ppermute | solution.py:18
  492.5 12.5 %collective-permute-start = (bf16[256,2,1,256]{3,0,2,1:T(8,128)(2,1)}, bf16[256,2,1,256]{3,0,2,1:T(8,128)(2,1)S(1)}, u32[]{:S(2)}, u32[]{:S(2)}) collective-permute-start(bf16[256,2,1,256]{3,0,2,1:T(8,128)(2,1)} %get-tuple-element.205), channel_id=1, source_target_pairs={{0,8},{8,16},{16,24},{24,32},{32,40},{40,48},{48,56},{56,64},{64,7... | collective-permute-start | bytes 786440 | tf_op jit(solution)/shard_map/while/body/eval_jaxpr/ppermute | solution.py:18
  495.1 7.5 %collective-permute-start.1 = (s32[256]{0:T(256)}, s32[256]{0:T(256)S(1)}, u32[]{:S(2)}, u32[]{:S(2)}) collective-permute-start(s32[256]{0:T(256)} %get-tuple-element.206), channel_id=1, source_target_pairs={{0,8},{8,16},{16,24},{24,32},{32,40},{40,48},{48,56},{56,64},{64,7... | collective-permute-start | bytes 3080 | tf_op jit(solution)/shard_map/while/body/eval_jaxpr/ppermute | solution.py:18
  505.8 12.5 %collective-permute-start = (bf16[256,2,1,256]{3,0,2,1:T(8,128)(2,1)}, bf16[256,2,1,256]{3,0,2,1:T(8,128)(2,1)S(1)}, u32[]{:S(2)}, u32[]{:S(2)}) collective-permute-start(bf16[256,2,1,256]{3,0,2,1:T(8,128)(2,1)} %get-tuple-element.205), channel_id=1, source_target_pairs={{0,8},{8,16},{16,24},{24,32},{32,40},{40,48},{48,56},{56,64},{64,7... | collective-permute-start | bytes 786440 | tf_op jit(solution)/shard_map/while/body/eval_jaxpr/ppermute | solution.py:18
  508.3 7.5 %collective-permute-start.1 = (s32[256]{0:T(256)}, s32[256]{0:T(256)S(1)}, u32[]{:S(2)}, u32[]{:S(2)}) collective-permute-start(s32[256]{0:T(256)} %get-tuple-element.206), channel_id=1, source_target_pairs={{0,8},{8,16},{16,24},{24,32},{32,40},{40,48},{48,56},{56,64},{64,7... | collective-permute-start | bytes 3080 | tf_op jit(solution)/shard_map/while/body/eval_jaxpr/ppermute | solution.py:18
  519.0 12.5 %collective-permute-start = (bf16[256,2,1,256]{3,0,2,1:T(8,128)(2,1)}, bf16[256,2,1,256]{3,0,2,1:T(8,128)(2,1)S(1)}, u32[]{:S(2)}, u32[]{:S(2)}) collective-permute-start(bf16[256,2,1,256]{3,0,2,1:T(8,128)(2,1)} %get-tuple-element.205), channel_id=1, source_target_pairs={{0,8},{8,16},{16,24},{24,32},{32,40},{40,48},{48,56},{56,64},{64,7... | collective-permute-start | bytes 786440 | tf_op jit(solution)/shard_map/while/body/eval_jaxpr/ppermute | solution.py:18
  521.6 7.5 %collective-permute-start.1 = (s32[256]{0:T(256)}, s32[256]{0:T(256)S(1)}, u32[]{:S(2)}, u32[]{:S(2)}) collective-permute-start(s32[256]{0:T(256)} %get-tuple-element.206), channel_id=1, source_target_pairs={{0,8},{8,16},{16,24},{24,32},{32,40},{40,48},{48,56},{56,64},{64,7... | collective-permute-start | bytes 3080 | tf_op jit(solution)/shard_map/while/body/eval_jaxpr/ppermute | solution.py:18
  532.2 12.5 %collective-permute-start = (bf16[256,2,1,256]{3,0,2,1:T(8,128)(2,1)}, bf16[256,2,1,256]{3,0,2,1:T(8,128)(2,1)S(1)}, u32[]{:S(2)}, u32[]{:S(2)}) collective-permute-start(bf16[256,2,1,256]{3,0,2,1:T(8,128)(2,1)} %get-tuple-element.205), channel_id=1, source_target_pairs={{0,8},{8,16},{16,24},{24,32},{32,40},{40,48},{48,56},{56,64},{64,7... | collective-permute-start | bytes 786440 | tf_op jit(solution)/shard_map/while/body/eval_jaxpr/ppermute | solution.py:18
  534.8 7.5 %collective-permute-start.1 = (s32[256]{0:T(256)}, s32[256]{0:T(256)S(1)}, u32[]{:S(2)}, u32[]{:S(2)}) collective-permute-start(s32[256]{0:T(256)} %get-tuple-element.206), channel_id=1, source_target_pairs={{0,8},{8,16},{16,24},{24,32},{32,40},{40,48},{48,56},{56,64},{64,7... | collective-permute-start | bytes 3080 | tf_op jit(solution)/shard_map/while/body/eval_jaxpr/ppermute | solution.py:18
  556.4 7.9 %collective-permute-start.3 = (bf16[128,2,1,256]{0,3,2,1:T(8,128)(2,1)S(1)}, bf16[128,2,1,256]{0,3,2,1:T(8,128)(2,1)S(1)}, u32[]{:S(2)}, u32[]{:S(2)}) collective-permute-start(bf16[128,2,1,256]{0,3,2,1:T(8,128)(2,1)S(1)} %slice.78), channel_id=1, source_target_pairs={{8,0},{16,8},{24,16},{32,24},{40,32},{48,40},{56,48},{64,56},{72,6... | collective-permute-start | bytes 393224 | tf_op jit(solution)/shard_map/ppermute | solution.py:18
  (16 other events, 281.6 us)
Sparse Core Ops, SparseCore 0:
  11.1 71.9 all-gather.1
  548.4 160.3 reduce-scatter.1
where the time goes:
time: 720 us; the launch traced here: 716 us
  starting transfers between devices  305 us (42%)
  waiting for transfers between devices  235 us (33%)
  local copies, waits for them, and re-layouts  89.6 us (12%)
  loops' own time  40.5 us (6%)
  matrix products  21.1 us (3%)
  between operations  14.2 us (2%)
  other arithmetic  10.4 us (1%)
    ppermute x66, starting transfers between devices, passed_along(): lax.ppermute(value, axis, [(source, source + steps) for source in range(f...  305 us
    reduce_scatter x1, waiting for transfers between devices, per_device(): lax.psum_scatter(partial_value.astype(jnp.bfloat16), 'tp', scatter_dimens...  139 us
    all_gather x1, waiting for transfers between devices, per_device(): whole_rows = lax.all_gather(hidden_in, 'tp', axis=1, tiled=True)  70.6 us
    while x64, local copies, waits for them, and re-layouts  41 us
    another operation x1, loops' own time, per_device(): lax.fori_loop(0, reach, relay_step, (pair_block, own_marks, carry_state))[2]  40.4 us
    ppermute x66, waiting for transfers between devices, passed_along(): lax.ppermute(value, axis, [(source, source + steps) for source in range(f...  23.9 us
    slice x32, local copies, waits for them, and re-layouts, visit_block(): tail_mark = key_marks[key_marks.shape[0] - 1]  20.7 us
    slice x32, local copies, waits for them, and re-layouts, visit_block(): relevant = tail_mark == query_marks[0]  16.2 us
  transfers between devices with their start and end apart: 68, of which 36 were waited for; matrix products, arithmetic and copies ran while one was open for 10% of the time, Pallas kernels for 0%

commit v1 on v0

v1 whole, which is shorter than its diff:
```python
import jax
import jax.numpy as jnp
from jax import lax
from jax.experimental import pallas as pl
from jax.experimental.pallas import tpu as pltpu
from jax.sharding import PartitionSpec as P

HD = 256
PAGE = 128
ROWS = 256
GROUP = 32
EPSILON = 1e-05
MESH = pl.DeviceIdType.MESH
F32 = jnp.float32
BF16 = jnp.bfloat16

OFFSETS = (0, -1, 1, 0, -2, 2, -1, 1, -3, 3, -2, 2, 4, -3, 3, -4)
CROSS = (3, 6, 7, 10, 11, 13, 14, 15)


def pick(step, table):
    value = 0
    for place, entry in enumerate(table):
        if entry != 0:
            value = value + jnp.where(step == place, entry, 0)
    return value


def among(step, places):
    found = step == places[0]
    for place in places[1:]:
        found = found | (step == place)
    return found


def remote(src, dst, send, recv, **where):
    return pltpu.make_async_remote_copy(
        src_ref=src, dst_ref=dst, send_sem=send, recv_sem=recv, device_id=where, device_id_type=MESH
    )


def kernel(
    lengths, pages, hidden, gain, bias, cosine, sine, w_qkv, w_out,
    out, cache,
    gathered, normed, w_qkv_v, w_out_v, queries, pairs, every, best, total, acc,
    helped, attended, terms, first, second, last,
    local_sem, ag_send, ag_recv, kv_send, kv_recv, extra_send, extra_recv, rs_send, rs_recv,
):
    ctx = lax.axis_index("ctx")
    tp = lax.axis_index("tp")
    group = ctx // GROUP
    local = ctx % GROUP
    z = local // 16
    y = (local // 2) % 8
    core = local % 2
    base = group * GROUP
    half = tp // 4
    x = tp % 4
    up = base + z * 16 + ((y + 1) % 8) * 2 + core
    down = base + z * 16 + ((y + 7) % 8) * 2 + core
    twin = base + z * 16 + y * 2 + (1 - core)
    across = base + (1 - z) * 16 + y * 2 + core
    x_up = half * 4 + (x + 1) % 4
    x_down = half * 4 + (x + 3) % 4
    x_far = half * 4 + (x + 2) % 4
    mirror = (1 - half) * 4 + x
    is_helper = ctx == 16
    is_helped = ctx == 32

    copies_in = [
        pltpu.make_async_copy(w_qkv, w_qkv_v, local_sem.at[0]),
        pltpu.make_async_copy(w_out, w_out_v, local_sem.at[1]),
    ]
    for copy in copies_in:
        copy.start()

    barrier = pltpu.get_barrier_semaphore()
    for peer in (up, down, twin, across):
        pl.semaphore_signal(barrier, inc=1, device_id={"ctx": peer}, device_id_type=MESH)
    for peer in (x_up, x_down, mirror):
        pl.semaphore_signal(barrier, inc=1, device_id={"tp": peer}, device_id_type=MESH)

    @pl.when(ctx > 0)
    def _():
        pl.semaphore_signal(barrier, inc=1, device_id={"ctx": ctx - 1}, device_id_type=MESH)

    @pl.when(ctx < 63)
    def _():
        pl.semaphore_signal(barrier, inc=1, device_id={"ctx": ctx + 1}, device_id_type=MESH)

    @pl.when(is_helper | is_helped)
    def _():
        pl.semaphore_signal(barrier, inc=1, device_id={"ctx": 48 - ctx}, device_id_type=MESH)

    pl.semaphore_wait(
        barrier,
        7 + jnp.where(ctx > 0, 1, 0) + jnp.where(ctx < 63, 1, 0)
        + jnp.where(is_helper | is_helped, 1, 0),
    )

    top, bottom = pl.ds(0, 128), pl.ds(128, 128)

    def feature_copy(number, src, slot, part, peer, rows=None):
        dst = gathered.at[slot] if rows is None else gathered.at[slot, rows]
        return remote(src, dst, ag_send.at[number], ag_recv.at[slot, part], tp=peer)

    own_z = feature_copy(0, hidden, tp, 0, mirror)
    own_up = feature_copy(1, hidden, tp, 0, x_up)
    own_down = feature_copy(2, hidden, tp, 0, x_down)
    for copy in (own_z, own_up, own_down):
        copy.start()
    gathered[tp] = hidden[...]
    sent = [own_z, own_up, own_down]

    def arrived(slot, part, rows=None):
        dst = gathered.at[slot] if rows is None else gathered.at[slot, rows]
        remote(dst, dst, ag_send.at[0], ag_recv.at[slot, part], tp=mirror).wait_recv()

    def pass_on(slot_down, slot_up, number):
        arrived(slot_down, 0)
        one = feature_copy(number, gathered.at[slot_down, top], slot_down, 0, x_up, top)
        one.start()
        arrived(slot_up, 0)
        two = feature_copy(number + 1, gathered.at[slot_up, bottom], slot_up, 1, x_down, bottom)
        two.start()
        sent.extend([one, two])

    pass_on(x_down, x_up, 3)
    other = (1 - half) * 4
    arrived(mirror, 0)
    cross_up = feature_copy(5, gathered.at[mirror], mirror, 0, x_up)
    cross_down = feature_copy(6, gathered.at[mirror], mirror, 0, x_down)
    cross_up.start()
    cross_down.start()
    sent.extend([cross_up, cross_down])
    arrived(x_far, 0, top)
    arrived(x_far, 1, bottom)
    pass_on(other + (x + 3) % 4, other + (x + 1) % 4, 7)
    arrived(other + (x + 2) % 4, 0, top)
    arrived(other + (x + 2) % 4, 1, bottom)
    for copy in sent:
        copy.wait_send()

    @pl.loop(0, ROWS // 32)
    def _(step):
        rows = pl.ds(pl.multiple_of(step * 32, 32), 32)
        blocks = [gathered[b, rows, :].astype(F32) for b in range(8)]
        average = jnp.sum(sum(blocks), axis=-1, keepdims=True) / 2048
        centered = [block - average for block in blocks]
        spread = jnp.sum(sum(c * c for c in centered), axis=-1, keepdims=True) / 2048
        scale = lax.rsqrt(spread + EPSILON)
        for b in range(8):
            cols = pl.ds(b * 256, 256)
            value = centered[b] * scale * gain[:, cols] + bias[:, cols]
            normed[rows, cols] = value.astype(BF16)

    copies_in[0].wait()
    lane = lax.broadcasted_iota(jnp.int32, (ROWS, 128), 1)

    def turn(value):
        lead = value[:, :128]
        turned = jnp.where(lane < 32, pltpu.roll(lead, 96, 1), pltpu.roll(lead, 32, 1))
        lead = lead * cosine[...] + turned * sine[...]
        return jnp.concatenate([lead, value[:, 128:]], axis=1).astype(BF16)

    key = turn(jnp.dot(normed[...], w_qkv_v[1], preferred_element_type=F32))
    pairs[local, :, 0:256] = key
    every[0:256, 0:256] = key
    value = jnp.dot(normed[...], w_qkv_v[2], preferred_element_type=F32).astype(BF16)
    pairs[local, :, 256:512] = value
    every[0:256, 256:512] = value

    def pair_copy(way, slot, peer):
        return remote(
            pairs.at[slot], pairs.at[slot], kv_send.at[way, slot], kv_recv.at[slot], ctx=peer
        )

    pair_copy(0, local, up).start()
    pair_copy(1, local, down).start()

    @pl.when(z == 0)
    def _():
        pair_copy(2, local, across).start()

    pair_copy(3, local, twin).start()
    tail = remote(
        pairs.at[local, pl.ds(0, PAGE)], every.at[pl.ds(256, PAGE)],
        extra_send.at[0], extra_recv.at[0], ctx=jnp.maximum(ctx - 1, 0),
    )

    @pl.when(ctx > 0)
    def _():
        tail.start()

    query = turn(jnp.dot(normed[...], w_qkv_v[0], preferred_element_type=F32))
    queries[0] = query * jnp.asarray(1 / 16, BF16)

    ask = remote(queries.at[0], queries.at[1], extra_send.at[1], extra_recv.at[1], ctx=16)
    show = remote(pairs.at[local], pairs.at[GROUP], extra_send.at[2], extra_recv.at[2], ctx=16)
    give = remote(helped.at[0], helped.at[1], extra_send.at[3], extra_recv.at[3], ctx=32)

    @pl.when(is_helped)
    def _():
        ask.start()
        show.start()

    best[...] = jnp.full(best.shape, -jnp.inf, F32)
    total[...] = jnp.zeros(total.shape, F32)
    acc[...] = jnp.zeros(acc.shape, F32)
    length = lengths[0]
    q_place = lax.broadcasted_iota(jnp.int32, (ROWS, ROWS), 0)
    k_place = lax.broadcasted_iota(jnp.int32, (ROWS, ROWS), 1)

    def attend(which, slot, visible):
        scores = lax.dot_general(
            queries[which], pairs[slot, :, 0:256], (((1,), (1,)), ((), ())),
            preferred_element_type=F32,
        )
        scores = jnp.where(visible, scores, -jnp.inf)
        before = best[which]
        newest = jnp.maximum(before, jnp.max(scores, axis=-1, keepdims=True))
        rescale = jnp.exp(before - newest)
        weights = jnp.exp(scores - jnp.concatenate([newest, newest], axis=1)).astype(BF16)
        total[which] = total[which] * rescale + jnp.sum(
            weights.astype(F32), axis=-1, keepdims=True
        )
        acc[which] = acc[which] * jnp.concatenate([rescale, rescale], axis=1) + jnp.dot(
            weights, pairs[slot, :, 256:512], preferred_element_type=F32
        )
        best[which] = newest

    def visit(slot):
        bound = jnp.where(slot == 0, length, 0)

        def one(which, carry):
            attend(which, slot, k_place >= bound)
            return carry

        lax.fori_loop(
            jnp.where(slot < local, 0, 1), jnp.where(is_helper, 2, 1), one, 0
        )

    own_bound = jnp.where(local == 0, length, 0)
    causal = k_place <= q_place
    attend(0, local, causal & ((k_place >= own_bound) == (q_place >= own_bound)))

    def here(slot):
        pair_copy(0, slot, up).wait_recv()

    @pl.when(is_helper)
    def _():
        ask.wait_recv()
        show.wait_recv()
        attend(1, GROUP, causal)
        visit(local)

    @pl.when(ctx < 63)
    def _():
        tail.wait_recv()

    @pl.when(ctx == 63)
    def _():
        every[256:384, :] = jnp.zeros((PAGE, 512), BF16)

    shifts = [0] * 5
    counts = [0] * 5
    start = 0
    token = ctx * ROWS
    for prompt in range(3):
        size = lengths[prompt]
        head = jnp.maximum(token - start + PAGE - 1, 0) // PAGE
        for number in range(2):
            page = head + number
            row = start + page * PAGE - token
            valid = (row < ROWS) & (page * PAGE < size)
            entry = pages[prompt, jnp.minimum(page, 63)] % 5
            for slot in range(5):
                hit = valid & (entry == slot)
                shifts[slot] = shifts[slot] + jnp.where(hit, row, 0)
                counts[slot] = counts[slot] + jnp.where(hit, jnp.minimum(size - page * PAGE, PAGE), 0)
        start = start + size
    to_row = lax.broadcasted_iota(jnp.int32, (PAGE, 384), 0)
    from_row = lax.broadcasted_iota(jnp.int32, (PAGE, 384), 1)
    for slot in range(5):
        placing = (from_row == to_row + shifts[slot]) & (to_row < counts[slot])
        placing = jnp.where(placing, 1.0, 0.0).astype(BF16)
        cache[slot] = jnp.dot(placing, every[...], preferred_element_type=F32).astype(BF16)

    here(local + 1 - 2 * core)
    visit(local + 1 - 2 * core)

    def event(step, carry):
        crossing = among(step, CROSS)
        row = jnp.where(crossing, 0, z)
        spot = row * 16 + ((y + pick(step, OFFSETS) + 8) % 8) * 2

        @pl.when((z == 1) | jnp.logical_not(crossing))
        def _():
            slot = spot + core
            here(slot)

            @pl.when(goes_up(step))
            def _():
                pair_copy(0, slot, up).start()

            @pl.when(goes_down(step))
            def _():
                pair_copy(1, slot, down).start()

            @pl.when(goes_across(step))
            def _():
                pair_copy(2, slot, across).start()

            pair_copy(3, slot, twin).start()
            visit(slot)
            beside = spot + 1 - core
            here(beside)
            visit(beside)

        return carry

    def goes_up(step):
        return among(step, (1, 4, 10, 13)) | ((step == 8) & (z == 0))

    def goes_down(step):
        return among(step, (2, 5, 11)) | ((step == 9) & (z == 1))

    def goes_across(step):
        return among(step, (1, 2, 4, 5)) & (z == 0)

    lax.fori_loop(1, 16, event, 0)

    @pl.when(is_helper)
    def _():
        helped[0] = (acc[1] / jnp.concatenate([total[1], total[1]], axis=1)).astype(BF16)
        give.start()

    result = (acc[0] / jnp.concatenate([total[0], total[0]], axis=1)).astype(BF16)
    attended[...] = result

    @pl.when(is_helped)
    def _():
        give.wait_recv()
        rows = lax.broadcasted_iota(jnp.int32, (ROWS, 256), 0)
        merged = jnp.where(rows < length, helped[1].astype(F32), attended[...].astype(F32))
        attended[...] = merged.astype(BF16)

    copies_in[1].wait()

    @pl.loop(0, 8)
    def _(b):
        cols = pl.ds(pl.multiple_of(b * 256, 256), 256)
        terms[b] = jnp.dot(
            attended[...], w_out_v[:, cols], preferred_element_type=F32
        ).astype(BF16)

    def sum_copy(number, src, dst, peer):
        return remote(src, dst, rs_send.at[number], rs_recv.at[number], tp=peer)

    first_ups, first_downs = [], []
    for k in range(2):
        side = (1 - half if k == 0 else half) * 4
        far = side + (x + 2) % 4
        first_ups.append(sum_copy(4 * k, terms.at[far, top], first.at[k, top], x_up))
        first_downs.append(
            sum_copy(4 * k + 1, terms.at[far, bottom], first.at[k, bottom], x_down)
        )
        first_ups[k].start()
        first_downs[k].start()
    seconds = []
    for k in range(2):
        side = (1 - half if k == 0 else half) * 4
        to_up, to_down = side + (x + 1) % 4, side + (x + 3) % 4
        first_ups[k].wait_recv()
        terms[to_up, top] = (
            terms[to_up, top].astype(F32) + first[k, top].astype(F32)
        ).astype(BF16)
        one = sum_copy(4 * k + 2, terms.at[to_up], second.at[k, 0], x_up)
        one.start()
        first_downs[k].wait_recv()
        terms[to_down, bottom] = (
            terms[to_down, bottom].astype(F32) + first[k, bottom].astype(F32)
        ).astype(BF16)
        two = sum_copy(4 * k + 3, terms.at[to_down], second.at[k, 1], x_down)
        two.start()
        seconds.append((one, two))

    def summed(k):
        side = (1 - half if k == 0 else half) * 4
        for copy in seconds[k]:
            copy.wait_recv()
        return (
            terms[side + x].astype(F32) + second[k, 0].astype(F32) + second[k, 1].astype(F32)
        )

    last[0] = summed(0).astype(BF16)
    final = sum_copy(8, last.at[0], last.at[1], mirror)
    final.start()
    kept = summed(1)
    final.wait_recv()
    out[...] = (kept + last[1].astype(F32)).astype(BF16)

    for copy in first_ups + first_downs + [c for pair in seconds for c in pair] + [final]:
        copy.wait_send()

    @pl.when(ctx > 0)
    def _():
        tail.wait_send()

    @pl.when(is_helped)
    def _():
        ask.wait_send()
        show.wait_send()

    @pl.when(is_helper)
    def _():
        give.wait_send()

    pair_copy(0, local, up).wait_send()
    pair_copy(1, local, down).wait_send()

    @pl.when(z == 0)
    def _():
        pair_copy(2, local, across).wait_send()

    pair_copy(3, local, twin).wait_send()

    def drain(step, carry):
        crossing = among(step, CROSS)
        row = jnp.where(crossing, 0, z)
        slot = row * 16 + ((y + pick(step, OFFSETS) + 8) % 8) * 2 + core

        @pl.when((z == 1) | jnp.logical_not(crossing))
        def _():
            @pl.when(goes_up(step))
            def _():
                pair_copy(0, slot, up).wait_send()

            @pl.when(goes_down(step))
            def _():
                pair_copy(1, slot, down).wait_send()

            @pl.when(goes_across(step))
            def _():
                pair_copy(2, slot, across).wait_send()

            pair_copy(3, slot, twin).wait_send()

        return carry

    lax.fori_loop(1, 16, drain, 0)


def rotary_tables(prompt_lengths):
    quarter = HD // 4
    exponent = jnp.arange(0, quarter, 2).astype(F32) / quarter
    inverse = jnp.power(F32(10000.0), -exponent)
    index = lax.axis_index("ctx") * ROWS + jnp.arange(ROWS, dtype=jnp.int32)
    first, both = prompt_lengths[0], prompt_lengths[0] + prompt_lengths[1]
    start = jnp.where(index < first, 0, jnp.where(index < both, first, both))
    angles = (index - start).astype(F32)[:, None] * inverse[None, :]
    cosine, sine = jnp.cos(angles), jnp.sin(angles)
    ones, zeros = jnp.ones((ROWS, 64), F32), jnp.zeros((ROWS, 64), F32)
    return (
        jnp.concatenate([cosine, cosine, ones], axis=1),
        jnp.concatenate([-sine, sine, zeros], axis=1),
    )


def per_device(hidden_in, ln_gain, ln_bias, w_qkv, w_out, segment_ids, prompt_lengths, page_table):
    cosine, sine = rotary_tables(prompt_lengths)
    vmem = pl.BlockSpec(memory_space=pltpu.VMEM)
    smem = pl.BlockSpec(memory_space=pltpu.SMEM)
    held = pl.BlockSpec(memory_space=pl.ANY)
    dma = pltpu.SemaphoreType.DMA
    attn_out, cache = pl.pallas_call(
        kernel,
        out_shape=(
            jax.ShapeDtypeStruct((ROWS, 256), BF16),
            jax.ShapeDtypeStruct((5, PAGE, 512), BF16),
        ),
        in_specs=[smem, smem, vmem, vmem, vmem, vmem, vmem, held, held],
        out_specs=(vmem, vmem),
        scratch_shapes=[
            pltpu.VMEM((8, ROWS, 256), BF16),
            pltpu.VMEM((ROWS, 2048), BF16),
            pltpu.VMEM((3, 2048, 256), BF16),
            pltpu.VMEM((256, 2048), BF16),
            pltpu.VMEM((2, ROWS, 256), BF16),
            pltpu.VMEM((GROUP + 1, ROWS, 512), BF16),
            pltpu.VMEM((384, 512), BF16),
            pltpu.VMEM((2, ROWS, 128), F32),
            pltpu.VMEM((2, ROWS, 128), F32),
            pltpu.VMEM((2, ROWS, 256), F32),
            pltpu.VMEM((2, ROWS, 256), BF16),
            pltpu.VMEM((ROWS, 256), BF16),
            pltpu.VMEM((8, ROWS, 256), BF16),
            pltpu.VMEM((2, ROWS, 256), BF16),
            pltpu.VMEM((2, 2, ROWS, 256), BF16),
            pltpu.VMEM((2, ROWS, 256), BF16),
            dma((2,)),
            dma((9,)),
            dma((8, 2)),
            dma((4, GROUP)),
            dma((GROUP,)),
            dma((4,)),
            dma((4,)),
            dma((9,)),
            dma((9,)),
        ],
        compiler_params=pltpu.CompilerParams(
            collective_id=0, has_side_effects=True, vmem_limit_bytes=44 * 1024 * 1024
        ),
    )(
        prompt_lengths, page_table, hidden_in, ln_gain.reshape(1, -1), ln_bias.reshape(1, -1),
        cosine, sine, w_qkv, w_out,
    )
    return (attn_out, cache.reshape(5, PAGE, 2, 256))


def solution(mesh):
    return jax.shard_map(
        per_device,
        mesh=mesh,
        in_specs=(P("ctx", "tp"), P(), P(), P(None, None, "tp"), P("tp", None), P("ctx"), P(), P()),
        out_specs=(P("ctx", "tp"), P("ctx", None, None, "tp")),
        check_vma=False,
    )
```

time: 720 us -> 113 us (0.16)
  the two profiles are of different devices: /device:TPU:16 before, /device:TPU:66 now
where the time goes in v1:
time: 113 us
  Pallas kernels  100 us (88%)
  local copies, waits for them, and re-layouts  9.86 us (9%)
  between operations  1.98 us (2%)
  other arithmetic  1.33 us (1%)
    pallas_call x1, Pallas kernels, per_device(): pl.pallas_call(kernel, out_shape=(jax.ShapeDtypeStruct((ROWS, 256), BF16)...  100 us
    unnamed x15, local copies, waits for them, and re-layouts  7.4 us

profile of v1, /device:TPU:66, one launch (start us, length us, event | category | flops | bytes accessed | tf_op | source)
XLA Modules:
  0.0 113.1 jit_solution(2561203407934045671)
XLA Ops:
  0.6 0.1 pad.5.clone
  0.7 0.1 pad.2.clone
  0.8 1.3 %fusion.3 = (s32[1]{0:T(128)}, s32[1]{0:T(128)}) fusion(s32[3]{0:T(128)} %lengths.1), kind=kLoop, calls=%fused_computation.10 | loop fusion | bytes 16 | tf_op jit(solution)/shard_map/slice | solution.py:459
  3.4 0.7 fusion.2
  4.1 0.5 fusion
  4.6 0.1 maximum_maximum_fusion
  4.8 0.0 copy-start
  4.8 1.9 %copy-done = bf16[3,2048,256]{2,1,0:T(8,128)(2,1)S(1)} copy-done((bf16[3,2048,256]{2,1,0:T(8,128)(2,1)S(1)}, bf16[3,2048,256]{2,1,0:T(8,128)(2,1)}, u32[]{:S(2)}) %copy-start) | copy-done | bytes 3145752
  6.7 0.0 copy-start.1
  6.7 1.2 %copy-done.1 = bf16[256,2048]{1,0:T(8,128)(2,1)S(1)} copy-done((bf16[256,2048]{1,0:T(8,128)(2,1)S(1)}, bf16[256,2048]{1,0:T(8,128)(2,1)}, u32[]{:S(2)}) %copy-start.1) | copy-done | bytes 1048600
  7.9 0.0 copy-start.2
  7.9 0.9 copy-done.2
  8.8 0.0 copy-start.3
  8.8 0.7 copy-done.3
  9.5 0.0 copy-start.4
  9.5 0.7 copy-done.4
  10.2 0.0 copy-start.5
  10.2 0.7 copy-done.5
  10.8 0.0 copy-start.6
  10.8 0.7 copy-done.6
  11.5 100.0 %shard_map.86 = (bf16[256,256]{1,0:T(8,128)(2,1)S(1)}, bf16[5,128,512]{2,1,0:T(8,128)(2,1)S(1)}) custom-call(s32[3]{0:T(128)S(1)} %copy-done.5, s32[3,64]{1,0:T(4,128)S(1)} %copy-done.6, bf16[256,256]{1,0:T(8,128)(2,1)S(1)} %copy-done.2, f32[1,2048]{1,0:T(1,128)S(1)} %bitcast.4, f32[1,2048]{1,0:T(1,128)S(1)} %bitcast.5, ...), custom_call_target="tpu_custom_call" | custom-call | tf_op jit(solution)/shard_map/pallas_call | solution.py:476
  111.5 1.0 reshape.33
  112.5 0.7 copy.11
  (3 shorter events, 0.0 us)
Async XLA Ops:
  4.8 1.9 %copy-start = (bf16[3,2048,256]{2,1,0:T(8,128)(2,1)S(1)}, bf16[3,2048,256]{2,1,0:T(8,128)(2,1)}, u32[]{:S(2)}) copy-start(bf16[3,2048,256]{2,1,0:T(8,128)(2,1)} %w_qkv.1) | copy-start | bytes 9437188
  6.7 1.2 %copy-start.1 = (bf16[256,2048]{1,0:T(8,128)(2,1)S(1)}, bf16[256,2048]{1,0:T(8,128)(2,1)}, u32[]{:S(2)}) copy-start(bf16[256,2048]{1,0:T(8,128)(2,1)} %w_out.1) | copy-start | bytes 3145732
  7.9 0.9 copy-start.2
  8.8 0.7 copy-start.3
  9.5 0.7 copy-start.4
  10.2 0.7 copy-start.5
  10.8 0.7 copy-start.6

commit v2 on v1

--- a/solution.py
+++ b/solution.py
@@ -1,4 +1,5 @@
 import jax
+import numpy as np
 import jax.numpy as jnp
 from jax import lax
 from jax.experimental import pallas as pl
@@ -10,6 +11,7 @@
 ROWS = 256
 GROUP = 32
 EPSILON = 1e-05
+TURN = (6.28125, 0.00193500518798828125, 3.0197e-07)
 MESH = pl.DeviceIdType.MESH
 F32 = jnp.float32
 BF16 = jnp.bfloat16
@@ -40,9 +42,9 @@
 
 
 def kernel(
-    lengths, pages, hidden, gain, bias, cosine, sine, w_qkv, w_out,
+    lengths, pages, hidden_h, gain_h, bias_h, inverse_h, w_qkv, w_out,
     out, cache,
-    gathered, normed, w_qkv_v, w_out_v, queries, pairs, every, best, total, acc,
+    hidden, gain, bias, inverse, cosine, sine, gathered, normed, w_qkv_v, w_out_v, queries, pairs, every, best, total, acc,
     helped, attended, terms, first, second, last,
     local_sem, ag_send, ag_recv, kv_send, kv_recv, extra_send, extra_recv, rs_send, rs_recv,
 ):
@@ -68,8 +70,11 @@
     is_helped = ctx == 32
 
     copies_in = [
-        pltpu.make_async_copy(w_qkv, w_qkv_v, local_sem.at[0]),
-        pltpu.make_async_copy(w_out, w_out_v, local_sem.at[1]),
+        pltpu.make_async_copy(source, target, local_sem.at[number])
+        for number, (source, target) in enumerate((
+            (hidden_h, hidden), (inverse_h, inverse), (gain_h, gain), (bias_h, bias),
+            (w_qkv, w_qkv_v), (w_out, w_out_v),
+        ))
     ]
     for copy in copies_in:
         copy.start()
@@ -104,6 +109,7 @@
         dst = gathered.at[slot] if rows is None else gathered.at[slot, rows]
         return remote(src, dst, ag_send.at[number], ag_recv.at[slot, part], tp=peer)
 
+    copies_in[0].wait()
     own_z = feature_copy(0, hidden, tp, 0, mirror)
     own_up = feature_copy(1, hidden, tp, 0, x_up)
     own_down = feature_copy(2, hidden, tp, 0, x_down)
@@ -111,6 +117,21 @@
         copy.start()
     gathered[tp] = hidden[...]
     sent = [own_z, own_up, own_down]
+
+    copies_in[1].wait()
+    index = ctx * ROWS + lax.broadcasted_iota(jnp.int32, (ROWS, 128), 0)
+    lane = lax.broadcasted_iota(jnp.int32, (ROWS, 128), 1)
+    length = lengths[0]
+    both = length + lengths[1]
+    places = index - jnp.where(index < length, 0, jnp.where(index < both, length, both))
+    angles = places.astype(F32) * inverse[...]
+    turns = jnp.floor(angles * F32(0.15915494309189535) + 0.5)
+    for part in TURN:
+        angles = angles - turns * F32(part)
+    cosine[...] = jnp.where(lane < 64, jnp.cos(angles), 1.0)
+    sine[...] = jnp.where(
+        lane < 32, -jnp.sin(angles), jnp.where(lane < 64, jnp.sin(angles), 0.0)
+    )
 
     def arrived(slot, part, rows=None):
         dst = gathered.at[slot] if rows is None else gathered.at[slot, rows]
@@ -141,6 +162,8 @@
     for copy in sent:
         copy.wait_send()
 
+    copies_in[2].wait()
+    copies_in[3].wait()
     @pl.loop(0, ROWS // 32)
     def _(step):
         rows = pl.ds(pl.multiple_of(step * 32, 32), 32)
@@ -154,8 +177,7 @@
             value = centered[b] * scale * gain[:, cols] + bias[:, cols]
             normed[rows, cols] = value.astype(BF16)
 
-    copies_in[0].wait()
-    lane = lax.broadcasted_iota(jnp.int32, (ROWS, 128), 1)
+    copies_in[4].wait()
 
     def turn(value):
         lead = value[:, :128]
@@ -207,7 +229,6 @@
     best[...] = jnp.full(best.shape, -jnp.inf, F32)
     total[...] = jnp.zeros(total.shape, F32)
     acc[...] = jnp.zeros(acc.shape, F32)
-    length = lengths[0]
     q_place = lax.broadcasted_iota(jnp.int32, (ROWS, ROWS), 0)
     k_place = lax.broadcasted_iota(jnp.int32, (ROWS, ROWS), 1)
 
@@ -345,7 +366,7 @@
         merged = jnp.where(rows < length, helped[1].astype(F32), attended[...].astype(F32))
         attended[...] = merged.astype(BF16)
 
-    copies_in[1].wait()
+    copies_in[5].wait()
 
     @pl.loop(0, 8)
     def _(b):
@@ -451,24 +472,9 @@
     lax.fori_loop(1, 16, drain, 0)
 
 
-def rotary_tables(prompt_lengths):
-    quarter = HD // 4
-    exponent = jnp.arange(0, quarter, 2).astype(F32) / quarter
-    inverse = jnp.power(F32(10000.0), -exponent)
-    index = lax.axis_index("ctx") * ROWS + jnp.arange(ROWS, dtype=jnp.int32)
-    first, both = prompt_lengths[0], prompt_lengths[0] + prompt_lengths[1]
-    start = jnp.where(index < first, 0, jnp.where(index < both, first, both))
-    angles = (index - start).astype(F32)[:, None] * inverse[None, :]
-    cosine, sine = jnp.cos(angles), jnp.sin(angles)
-    ones, zeros = jnp.ones((ROWS, 64), F32), jnp.zeros((ROWS, 64), F32)
-    return (
-        jnp.concatenate([cosine, cosine, ones], axis=1),
-        jnp.concatenate([-sine, sine, zeros], axis=1),
-    )
-
-
 def per_device(hidden_in, ln_gain, ln_bias, w_qkv, w_out, segment_ids, prompt_lengths, page_table):
-    cosine, sine = rotary_tables(prompt_lengths)
+    inverse = np.float32(10000.0) ** -(np.arange(0, 64, 2, dtype=np.float32) / np.float32(64))
+    inverse = np.tile(inverse.astype(np.float32), 4)[None, :]
     vmem = pl.BlockSpec(memory_space=pltpu.VMEM)
     smem = pl.BlockSpec(memory_space=pltpu.SMEM)
     held = pl.BlockSpec(memory_space=pl.ANY)
@@ -479,9 +485,15 @@
             jax.ShapeDtypeStruct((ROWS, 256), BF16),
             jax.ShapeDtypeStruct((5, PAGE, 512), BF16),
         ),
-        in_specs=[smem, smem, vmem, vmem, vmem, vmem, vmem, held, held],
+        in_specs=[smem, smem] + [held] * 6,
         out_specs=(vmem, vmem),
         scratch_shapes=[
+            pltpu.VMEM((ROWS, 256), BF16),
+            pltpu.VMEM((1, 2048), F32),
+            pltpu.VMEM((1, 2048), F32),
+            pltpu.VMEM((1, 128), F32),
+            pltpu.VMEM((ROWS, 128), F32),
+            pltpu.VMEM((ROWS, 128), F32),
             pltpu.VMEM((8, ROWS, 256), BF16),
             pltpu.VMEM((ROWS, 2048), BF16),
             pltpu.VMEM((3, 2048, 256), BF16),
@@ -498,7 +510,7 @@
             pltpu.VMEM((2, ROWS, 256), BF16),
             pltpu.VMEM((2, 2, ROWS, 256), BF16),
             pltpu.VMEM((2, ROWS, 256), BF16),
-            dma((2,)),
+            dma((6,)),
             dma((9,)),
             dma((8, 2)),
             dma((4, GROUP)),
@@ -509,11 +521,11 @@
             dma((9,)),
         ],
         compiler_params=pltpu.CompilerParams(
-            collective_id=0, has_side_effects=True, vmem_limit_bytes=44 * 1024 * 1024
+            collective_id=0, has_side_effects=True, vmem_limit_bytes=62 * 1024 * 1024
         ),
     )(
         prompt_lengths, page_table, hidden_in, ln_gain.reshape(1, -1), ln_bias.reshape(1, -1),
-        cosine, sine, w_qkv, w_out,
+        jnp.asarray(inverse), w_qkv, w_out,
     )
     return (attn_out, cache.reshape(5, PAGE, 2, 256))
 

time: 113 us -> 106 us (0.938)
  local copies, waits for them, and re-layouts: 9.86 us -> 4.25 us
  between operations: 1.98 us -> 0.64 us
  other arithmetic: 1.33 us -> 0 us
    unnamed x15 -> x1, local copies, waits for them, and re-layouts: 7.4 us -> 1.57 us
    reshape x1, local copies, waits for them, and re-layouts: 0.99 us -> 2.68 us  [per_device(): return (attn_out, cache.reshape(5, PAGE, 2, 256))]
    slice x1 -> x0, local copies, waits for them, and re-layouts: 1.32 us -> none  [rotary_tables(): first, both = (prompt_lengths[0], prompt_lengths[0] + prompt_lengths[1])]
where the time goes in v2:
time: 106 us
  Pallas kernels  101 us (95%)
  local copies, waits for them, and re-layouts  4.25 us (4%)
    pallas_call x1, Pallas kernels, per_device(): pl.pallas_call(kernel, out_shape=(jax.ShapeDtypeStruct((ROWS, 256), BF16)...  101 us
    reshape x1, local copies, waits for them, and re-layouts, per_device(): return (attn_out, cache.reshape(5, PAGE, 2, 256))  2.68 us

profile of v2, /device:TPU:66, one launch (start us, length us, event | category | flops | bytes accessed | tf_op | source)
XLA Modules:
  0.0 105.6 jit_solution(11760422308870143473)
XLA Ops:
  0.6 100.7 %shard_map.95 = (bf16[256,256]{1,0:T(8,128)(2,1)}, bf16[5,128,512]{2,1,0:T(8,128)(2,1)}) custom-call(s32[3]{0:T(128)} %lengths.1, s32[3,64]{1,0:T(4,128)} %pages.1, bf16[256,256]{1,0:T(8,128)(2,1)} %hidden_h.1, f32[1,2048]{1,0:T(1,128)} %bitcast.2, f32[1,2048]{1,0:T(1,128)} %bitcast.3, f32[1,128]{1,0:T(1,128)} %constant.2.clone.inverse_h, ...), custom_call_target="tpu_custom_call" | custom-call | tf_op jit(solution)/shard_map/pallas_call | solution.py:482
  101.4 2.7 %reshape.15 = bf16[5,128,2,256]{3,2,1,0:T(2,128)(2,1)} reshape(bf16[5,128,512]{2,1,0:T(8,128)(2,1)} %get-tuple-element.5) | data formatting | bytes 1310720 | tf_op jit(solution)/shard_map/reshape | solution.py:530
  104.0 1.6 %copy.11 = bf16[256,256]{1,0:T(8,128)(2,1)} copy(bf16[256,256]{1,0:T(8,128)(2,1)} %get-tuple-element.8) | data formatting | bytes 262144

commit v3 on v2

--- a/solution.py
+++ b/solution.py
@@ -16,8 +16,7 @@
 F32 = jnp.float32
 BF16 = jnp.bfloat16
 
-OFFSETS = (0, -1, 1, 0, -2, 2, -1, 1, -3, 3, -2, 2, 4, -3, 3, -4)
-CROSS = (3, 6, 7, 10, 11, 13, 14, 15)
+OFFSETS = (0, -1, 1, -2, 2, -3, 3)
 
 
 def pick(step, table):
@@ -28,13 +27,6 @@
     return value
 
 
-def among(step, places):
-    found = step == places[0]
-    for place in places[1:]:
-        found = found | (step == place)
-    return found
-
-
 def remote(src, dst, send, recv, **where):
     return pltpu.make_async_remote_copy(
         src_ref=src, dst_ref=dst, send_sem=send, recv_sem=recv, device_id=where, device_id_type=MESH
@@ -45,8 +37,8 @@
     lengths, pages, hidden_h, gain_h, bias_h, inverse_h, w_qkv, w_out,
     out, cache,
     hidden, gain, bias, inverse, cosine, sine, gathered, normed, w_qkv_v, w_out_v, queries, pairs, every, best, total, acc,
-    helped, attended, terms, first, second, last,
-    local_sem, ag_send, ag_recv, kv_send, kv_recv, extra_send, extra_recv, rs_send, rs_recv,
+    reply, weight, attended, terms, first, second, last,
+    local_sem, ag_send, ag_recv, kv_send, kv_recv, far_send, far_recv, extra_send, extra_recv, rs_send, rs_recv,
 ):
     ctx = lax.axis_index("ctx")
     tp = lax.axis_index("tp")
@@ -66,7 +58,8 @@
     x_down = half * 4 + (x + 3) % 4
     x_far = half * 4 + (x + 2) % 4
     mirror = (1 - half) * 4 + x
-    is_helper = ctx == 16
+    place = local % 16
+    is_helper = (ctx == 0) | (ctx == 16)
     is_helped = ctx == 32
 
     copies_in = [
@@ -93,14 +86,19 @@
     def _():
         pl.semaphore_signal(barrier, inc=1, device_id={"ctx": ctx + 1}, device_id_type=MESH)
 
-    @pl.when(is_helper | is_helped)
-    def _():
-        pl.semaphore_signal(barrier, inc=1, device_id={"ctx": 48 - ctx}, device_id_type=MESH)
+    @pl.when(is_helper)
+    def _():
+        pl.semaphore_signal(barrier, inc=1, device_id={"ctx": 32}, device_id_type=MESH)
+
+    @pl.when(is_helped)
+    def _():
+        for peer in (0, 16):
+            pl.semaphore_signal(barrier, inc=1, device_id={"ctx": peer}, device_id_type=MESH)
 
     pl.semaphore_wait(
         barrier,
         7 + jnp.where(ctx > 0, 1, 0) + jnp.where(ctx < 63, 1, 0)
-        + jnp.where(is_helper | is_helped, 1, 0),
+        + jnp.where(is_helper, 1, 0) + jnp.where(is_helped, 2, 0),
     )
 
     top, bottom = pl.ds(0, 128), pl.ds(128, 128)
@@ -186,10 +184,10 @@
         return jnp.concatenate([lead, value[:, 128:]], axis=1).astype(BF16)
 
     key = turn(jnp.dot(normed[...], w_qkv_v[1], preferred_element_type=F32))
-    pairs[local, :, 0:256] = key
+    pairs[place, :, 0:256] = key
     every[0:256, 0:256] = key
     value = jnp.dot(normed[...], w_qkv_v[2], preferred_element_type=F32).astype(BF16)
-    pairs[local, :, 256:512] = value
+    pairs[place, :, 256:512] = value
     every[0:256, 256:512] = value
 
     def pair_copy(way, slot, peer):
@@ -197,16 +195,11 @@
             pairs.at[slot], pairs.at[slot], kv_send.at[way, slot], kv_recv.at[slot], ctx=peer
         )
 
-    pair_copy(0, local, up).start()
-    pair_copy(1, local, down).start()
-
-    @pl.when(z == 0)
-    def _():
-        pair_copy(2, local, across).start()
-
-    pair_copy(3, local, twin).start()
+    pair_copy(0, place, up).start()
+    pair_copy(1, place, down).start()
+    pair_copy(2, place, twin).start()
     tail = remote(
-        pairs.at[local, pl.ds(0, PAGE)], every.at[pl.ds(256, PAGE)],
+        pairs.at[place, pl.ds(0, PAGE)], every.at[pl.ds(256, PAGE)],
         extra_send.at[0], extra_recv.at[0], ctx=jnp.maximum(ctx - 1, 0),
     )
 
@@ -217,14 +210,31 @@
     query = turn(jnp.dot(normed[...], w_qkv_v[0], preferred_element_type=F32))
     queries[0] = query * jnp.asarray(1 / 16, BF16)
 
-    ask = remote(queries.at[0], queries.at[1], extra_send.at[1], extra_recv.at[1], ctx=16)
-    show = remote(pairs.at[local], pairs.at[GROUP], extra_send.at[2], extra_recv.at[2], ctx=16)
-    give = remote(helped.at[0], helped.at[1], extra_send.at[3], extra_recv.at[3], ctx=32)
+    def message(src, dst, number, peer):
+        return remote(src, dst, extra_send.at[number], extra_recv.at[number], ctx=peer)
+
+    ask = message(queries.at[0], queries.at[1], 1, across)
+    asks = [message(queries.at[0], queries.at[2], 2 + i, 16 * i) for i in range(2)]
+    show = message(pairs.at[place], pairs.at[16], 4, 16)
+    gives = [
+        message(reply.at[0], reply.at[2], 5, across),
+        message(weight.at[0], weight.at[2], 6, across),
+    ]
+    back = 7 + 2 * z
+    helps = [
+        remote(reply.at[1], reply.at[3 + z], extra_send.at[7], extra_recv.at[back], ctx=32),
+        remote(weight.at[1], weight.at[3 + z], extra_send.at[8], extra_recv.at[back + 1], ctx=32),
+    ]
+
+    @pl.when(z == 1)
+    def _():
+        ask.start()
 
     @pl.when(is_helped)
     def _():
-        ask.start()
+        asks[1].start()
         show.start()
+        asks[0].start()
 
     best[...] = jnp.full(best.shape, -jnp.inf, F32)
     total[...] = jnp.zeros(total.shape, F32)
@@ -251,29 +261,27 @@
         best[which] = newest
 
     def visit(slot):
-        bound = jnp.where(slot == 0, length, 0)
+        bound = jnp.where((slot == 0) & (z == 0), length, 0)
 
         def one(which, carry):
-            attend(which, slot, k_place >= bound)
+            @pl.when(
+                ((which == 0) & (slot < place))
+                | ((which == 1) & (z == 0))
+                | ((which == 2) & is_helper)
+            )
+            def _():
+                attend(which, slot, k_place >= bound)
+
             return carry
 
-        lax.fori_loop(
-            jnp.where(slot < local, 0, 1), jnp.where(is_helper, 2, 1), one, 0
-        )
+        lax.fori_loop(0, 3, one, 0)
 
     own_bound = jnp.where(local == 0, length, 0)
     causal = k_place <= q_place
-    attend(0, local, causal & ((k_place >= own_bound) == (q_place >= own_bound)))
+    attend(0, place, causal & ((k_place >= own_bound) == (q_place >= own_bound)))
 
     def here(slot):
         pair_copy(0, slot, up).wait_recv()
-
-    @pl.when(is_helper)
-    def _():
-        ask.wait_recv()
-        show.wait_recv()
-        attend(1, GROUP, causal)
-        visit(local)
 
     @pl.when(ctx < 63)
     def _():
@@ -307,64 +315,125 @@
         placing = jnp.where(placing, 1.0, 0.0).astype(BF16)
         cache[slot] = jnp.dot(placing, every[...], preferred_element_type=F32).astype(BF16)
 
-    here(local + 1 - 2 * core)
-    visit(local + 1 - 2 * core)
+    @pl.when(z == 0)
+    def _():
+        ask.wait_recv()
+
+    @pl.when(ctx == 0)
+    def _():
+        asks[0].wait_recv()
+
+    @pl.when(ctx == 16)
+    def _():
+        asks[1].wait_recv()
+        show.wait_recv()
+        attend(2, 16, causal)
+
+    visit(place)
+    here(place + 1 - 2 * core)
+    visit(place + 1 - 2 * core)
+
+    def spot(step):
+        return ((y + pick(step, OFFSETS) + 8) % 8) * 2
 
     def event(step, carry):
-        crossing = among(step, CROSS)
-        row = jnp.where(crossing, 0, z)
-        spot = row * 16 + ((y + pick(step, OFFSETS) + 8) % 8) * 2
-
-        @pl.when((z == 1) | jnp.logical_not(crossing))
+        slot = spot(step) + core
+        here(slot)
+
+        @pl.when((step == 1) | (step == 3))
         def _():
-            slot = spot + core
-            here(slot)
-
-            @pl.when(goes_up(step))
-            def _():
-                pair_copy(0, slot, up).start()
-
-            @pl.when(goes_down(step))
-            def _():
-                pair_copy(1, slot, down).start()
-
-            @pl.when(goes_across(step))
-            def _():
-                pair_copy(2, slot, across).start()
-
-            pair_copy(3, slot, twin).start()
-            visit(slot)
-            beside = spot + 1 - core
-            here(beside)
-            visit(beside)
-
+            pair_copy(0, slot, up).start()
+
+        @pl.when((step == 2) | (step == 4))
+        def _():
+            pair_copy(1, slot, down).start()
+
+        @pl.when(step == 5)
+        def _():
+            half_copy(0, slot, up).start()
+
+        @pl.when(step == 6)
+        def _():
+            half_copy(1, slot, down).start()
+
+        pair_copy(2, slot, twin).start()
+        visit(slot)
+        beside = spot(step) + 1 - core
+        here(beside)
+        visit(beside)
         return carry
 
-    def goes_up(step):
-        return among(step, (1, 4, 10, 13)) | ((step == 8) & (z == 0))
-
-    def goes_down(step):
-        return among(step, (2, 5, 11)) | ((step == 9) & (z == 1))
-
-    def goes_across(step):
-        return among(step, (1, 2, 4, 5)) & (z == 0)
-
-    lax.fori_loop(1, 16, event, 0)
+    def half_copy(way, slot, peer):
+        rows = pl.ds(way * 128, 128)
+        return remote(
+            pairs.at[slot, rows], pairs.at[slot, rows],
+            far_send.at[way], far_recv.at[way], ctx=peer,
+        )
+
+    lax.fori_loop(1, 7, event, 0)
+    opposite = ((y + 4) % 8) * 2
+    half_copy(0, opposite + core, up).wait_recv()
+    half_copy(1, opposite + core, down).wait_recv()
+    pair_copy(2, opposite + core, twin).start()
+    visit(opposite + core)
+    here(opposite + 1 - core)
+    visit(opposite + 1 - core)
+
+    def wide(value):
+        return jnp.concatenate([value, value], axis=1)
+
+    def hand_back(which, copies):
+        reply[which - 1] = (acc[which] / wide(total[which])).astype(BF16)
+        weight[which - 1] = jnp.transpose(best[which] + jnp.log(total[which]))[0:8]
+        for copy in copies:
+            copy.start()
+
+    @pl.when(z == 0)
+    def _():
+        hand_back(1, gives)
 
     @pl.when(is_helper)
     def _():
-        helped[0] = (acc[1] / jnp.concatenate([total[1], total[1]], axis=1)).astype(BF16)
-        give.start()
-
-    result = (acc[0] / jnp.concatenate([total[0], total[0]], axis=1)).astype(BF16)
-    attended[...] = result
+        hand_back(2, helps)
+
+    def logs(number):
+        return jnp.transpose(jnp.tile(weight[number], (16, 1)))
+
+    result = acc[0] / wide(total[0])
+    attended[...] = result.astype(BF16)
+
+    def blend(one, one_log, two, two_log):
+        most = jnp.maximum(one_log, two_log)
+        one_part, two_part = jnp.exp(one_log - most), jnp.exp(two_log - most)
+        share = one_part / (one_part + two_part)
+        other_share = two_part / (one_part + two_part)
+        return one * wide(share) + two * wide(other_share)
+
+    @pl.when(z == 1)
+    def _():
+        for copy in gives:
+            copy.wait_recv()
+        mixed = blend(
+            acc[0] / wide(total[0]), best[0] + jnp.log(total[0]), reply[2].astype(F32), logs(2)
+        )
+        attended[...] = mixed.astype(BF16)
 
     @pl.when(is_helped)
     def _():
-        give.wait_recv()
+        for number in range(2):
+            remote(
+                reply.at[1], reply.at[3 + number],
+                extra_send.at[7], extra_recv.at[7 + 2 * number], ctx=0,
+            ).wait_recv()
+            remote(
+                weight.at[1], weight.at[3 + number],
+                extra_send.at[8], extra_recv.at[8 + 2 * number], ctx=0,
+            ).wait_recv()
+        mixed = blend(reply[3].astype(F32), logs(3), reply[4].astype(F32), logs(4))
         rows = lax.broadcasted_iota(jnp.int32, (ROWS, 256), 0)
-        merged = jnp.where(rows < length, helped[1].astype(F32), attended[...].astype(F32))
-        attended[...] = merged.astype(BF16)
+        attended[...] = jnp.where(
+            rows < length, mixed, attended[...].astype(F32)
+        ).astype(BF16)
 
     copies_in[5].wait()
 
@@ -428,48 +497,38 @@
     def _():
         tail.wait_send()
 
+    @pl.when(z == 1)
+    def _():
+        ask.wait_send()
+
     @pl.when(is_helped)
     def _():
-        ask.wait_send()
-        show.wait_send()
+        for copy in asks + [show]:
+            copy.wait_send()
+
+    @pl.when(z == 0)
+    def _():
+        for copy in gives:
+            copy.wait_send()
 
     @pl.when(is_helper)
     def _():
-        give.wait_send()
-
-    pair_copy(0, local, up).wait_send()
-    pair_copy(1, local, down).wait_send()
-
-    @pl.when(z == 0)
-    def _():
-        pair_copy(2, local, across).wait_send()
-
-    pair_copy(3, local, twin).wait_send()
-
-    def drain(step, carry):
-        crossing = among(step, CROSS)
-        row = jnp.where(crossing, 0, z)
-        slot = row * 16 + ((y + pick(step, OFFSETS) + 8) % 8) * 2 + core
-
-        @pl.when((z == 1) | jnp.logical_not(crossing))
-        def _():
-            @pl.when(goes_up(step))
-            def _():
-                pair_copy(0, slot, up).wait_send()
-
-            @pl.when(goes_down(step))
-            def _():
-                pair_copy(1, slot, down).wait_send()
-
-            @pl.when(goes_across(step))
-            def _():
-                pair_copy(2, slot, across).wait_send()
-
-            pair_copy(3, slot, twin).wait_send()
-
-        return carry
-
-    lax.fori_loop(1, 16, drain, 0)
+        for copy in helps:
+            copy.wait_send()
+
+    pair_copy(0, place, up).wait_send()
+    pair_copy(1, place, down).wait_send()
+    pair_copy(2, place, twin).wait_send()
+    for step in range(1, 7):
+        slot = spot(step) + core
+        if step in (1, 3):
+            pair_copy(0, slot, up).wait_send()
+        if step in (2, 4):
+            pair_copy(1, slot, down).wait_send()
+        if step in (5, 6):
+            half_copy(step - 5, slot, up).wait_send()
+        pair_copy(2, slot, twin).wait_send()
+    pair_copy(2, opposite + core, twin).wait_send()
 
 
 def per_device(hidden_in, ln_gain, ln_bias, w_qkv, w_out, segment_ids, prompt_lengths, page_table):
@@ -498,13 +557,14 @@
             pltpu.VMEM((ROWS, 2048), BF16),
             pltpu.VMEM((3, 2048, 256), BF16),
             pltpu.VMEM((256, 2048), BF16),
-            pltpu.VMEM((2, ROWS, 256), BF16),
-            pltpu.VMEM((GROUP + 1, ROWS, 512), BF16),
+            pltpu.VMEM((3, ROWS, 256), BF16),
+            pltpu.VMEM((17, ROWS, 512), BF16),
             pltpu.VMEM((384, 512), BF16),
-            pltpu.VMEM((2, ROWS, 128), F32),
-            pltpu.VMEM((2, ROWS, 128), F32),
-            pltpu.VMEM((2, ROWS, 256), F32),
-            pltpu.VMEM((2, ROWS, 256), BF16),
+            pltpu.VMEM((3, ROWS, 128), F32),
+            pltpu.VMEM((3, ROWS, 128), F32),
+            pltpu.VMEM((3, ROWS, 256), F32),
+            pltpu.VMEM((5, ROWS, 256), BF16),
+            pltpu.VMEM((5, 8, 256), F32),
             pltpu.VMEM((ROWS, 256), BF16),
             pltpu.VMEM((8, ROWS, 256), BF16),
             pltpu.VMEM((2, ROWS, 256), BF16),
@@ -513,10 +573,12 @@
             dma((6,)),
             dma((9,)),
             dma((8, 2)),
-            dma((4, GROUP)),
-            dma((GROUP,)),
-            dma((4,)),
-            dma((4,)),
+            dma((3, 16)),
+            dma((16,)),
+            dma((2,)),
+            dma((2,)),
+            dma((11,)),
+            dma((11,)),
             dma((9,)),
             dma((9,)),
         ],

time: 106 us -> 94 us (0.89)
  the two profiles are of different devices: /device:TPU:66 before, /device:TPU:112 now
where the time goes in v3:
time: 94 us; the launch traced here: 93.8 us
  Pallas kernels  88.9 us (95%)
  local copies, waits for them, and re-layouts  4.25 us (5%)
    pallas_call x1, Pallas kernels, per_device(): pl.pallas_call(kernel, out_shape=(jax.ShapeDtypeStruct((ROWS, 256), BF16)...  88.9 us
    reshape x1, local copies, waits for them, and re-layouts, per_device(): return (attn_out, cache.reshape(5, PAGE, 2, 256))  2.68 us

profile of v3, /device:TPU:112, one launch (start us, length us, event | category | flops | bytes accessed | tf_op | source)
XLA Modules:
  0.0 93.8 jit_solution(11573279737021848807)
XLA Ops:
  0.6 88.9 %shard_map.95 = (bf16[256,256]{1,0:T(8,128)(2,1)}, bf16[5,128,512]{2,1,0:T(8,128)(2,1)}) custom-call(s32[3]{0:T(128)} %lengths.1, s32[3,64]{1,0:T(4,128)} %pages.1, bf16[256,256]{1,0:T(8,128)(2,1)} %hidden_h.1, f32[1,2048]{1,0:T(1,128)} %bitcast.2, f32[1,2048]{1,0:T(1,128)} %bitcast.3, f32[1,128]{1,0:T(1,128)} %constant.2.clone.inverse_h, ...), custom_call_target="tpu_custom_call" | custom-call | tf_op jit(solution)/shard_map/pallas_call | solution.py:541
  89.6 2.7 %reshape.15 = bf16[5,128,2,256]{3,2,1,0:T(2,128)(2,1)} reshape(bf16[5,128,512]{2,1,0:T(8,128)(2,1)} %get-tuple-element.5) | data formatting | bytes 1310720 | tf_op jit(solution)/shard_map/reshape | solution.py:592
  92.3 1.6 %copy.11 = bf16[256,256]{1,0:T(8,128)(2,1)} copy(bf16[256,256]{1,0:T(8,128)(2,1)} %get-tuple-element.8) | data formatting | bytes 262144

commit v4 on v3

--- a/solution.py
+++ b/solution.py
@@ -38,7 +38,7 @@
     out, cache,
     hidden, gain, bias, inverse, cosine, sine, gathered, normed, w_qkv_v, w_out_v, queries, pairs, every, best, total, acc,
     reply, weight, attended, terms, first, second, last,
-    local_sem, ag_send, ag_recv, kv_send, kv_recv, far_send, far_recv, extra_send, extra_recv, rs_send, rs_recv,
+    relay, relay_recv, local_sem, ag_send, ag_recv, kv_send, kv_recv, far_send, far_recv, extra_send, extra_recv, rs_send, rs_recv,
 ):
     ctx = lax.axis_index("ctx")
     tp = lax.axis_index("tp")
@@ -62,6 +62,11 @@
     is_helper = (ctx == 0) | (ctx == 16)
     is_helped = ctx == 32
 
+    def along_z(steps):
+        there = (half * 4 + ctx // 16 + steps) % 8
+        return {"ctx": (there % 4) * 16 + ctx % 16, "tp": (there // 4) * 4 + x}
+
+
     copies_in = [
         pltpu.make_async_copy(source, target, local_sem.at[number])
         for number, (source, target) in enumerate((
@@ -78,6 +83,9 @@
     for peer in (x_up, x_down, mirror):
         pl.semaphore_signal(barrier, inc=1, device_id={"tp": peer}, device_id_type=MESH)
 
+    for steps in (1, 3, 5, 7):
+        pl.semaphore_signal(barrier, inc=1, device_id=along_z(steps), device_id_type=MESH)
+
     @pl.when(ctx > 0)
     def _():
         pl.semaphore_signal(barrier, inc=1, device_id={"ctx": ctx - 1}, device_id_type=MESH)
@@ -97,7 +105,7 @@
 
     pl.semaphore_wait(
         barrier,
-        7 + jnp.where(ctx > 0, 1, 0) + jnp.where(ctx < 63, 1, 0)
+        11 + jnp.where(ctx > 0, 1, 0) + jnp.where(ctx < 63, 1, 0)
         + jnp.where(is_helper, 1, 0) + jnp.where(is_helped, 2, 0),
     )
 
@@ -108,13 +116,14 @@
         return remote(src, dst, ag_send.at[number], ag_recv.at[slot, part], tp=peer)
 
     copies_in[0].wait()
-    own_z = feature_copy(0, hidden, tp, 0, mirror)
+    own_z = feature_copy(0, hidden.at[top], tp, 0, mirror, top)
+    own_relay = remote(hidden.at[bottom], relay.at[0], ag_send.at[9], relay_recv.at[0], **along_z(7))
     own_up = feature_copy(1, hidden, tp, 0, x_up)
     own_down = feature_copy(2, hidden, tp, 0, x_down)
-    for copy in (own_z, own_up, own_down):
+    for copy in (own_z, own_relay, own_up, own_down):
         copy.start()
     gathered[tp] = hidden[...]
-    sent = [own_z, own_up, own_down]
+    sent = [own_z, own_relay, own_up, own_down]
 
     copies_in[1].wait()
     index = ctx * ROWS + lax.broadcasted_iota(jnp.int32, (ROWS, 128), 0)
@@ -135,28 +144,39 @@
         dst = gathered.at[slot] if rows is None else gathered.at[slot, rows]
         remote(dst, dst, ag_send.at[0], ag_recv.at[slot, part], tp=mirror).wait_recv()
 
-    def pass_on(slot_down, slot_up, number):
-        arrived(slot_down, 0)
-        one = feature_copy(number, gathered.at[slot_down, top], slot_down, 0, x_up, top)
-        one.start()
-        arrived(slot_up, 0)
-        two = feature_copy(number + 1, gathered.at[slot_up, bottom], slot_up, 1, x_down, bottom)
-        two.start()
-        sent.extend([one, two])
-
-    pass_on(x_down, x_up, 3)
+    def send(copy):
+        copy.start()
+        sent.append(copy)
+
+    own_relay.wait_recv()
+    origin = along_z(1)["tp"]
+    send(remote(
+        relay.at[0], gathered.at[origin, bottom], ag_send.at[10], ag_recv.at[origin, 1],
+        **along_z(5),
+    ))
+
+    arrived(x_down, 0)
+    send(feature_copy(3, gathered.at[x_down, top], x_down, 0, x_up, top))
+    arrived(x_up, 0)
+    send(feature_copy(4, gathered.at[x_up, bottom], x_up, 1, x_down, bottom))
     other = (1 - half) * 4
-    arrived(mirror, 0)
-    cross_up = feature_copy(5, gathered.at[mirror], mirror, 0, x_up)
-    cross_down = feature_copy(6, gathered.at[mirror], mirror, 0, x_down)
-    cross_up.start()
-    cross_down.start()
-    sent.extend([cross_up, cross_down])
-    arrived(x_far, 0, top)
-    arrived(x_far, 1, bottom)
-    pass_on(other + (x + 3) % 4, other + (x + 1) % 4, 7)
-    arrived(other + (x + 2) % 4, 0, top)
-    arrived(other + (x + 2) % 4, 1, bottom)
+    beyond_down, beyond_up = other + (x + 3) % 4, other + (x + 1) % 4
+    beyond_far = other + (x + 2) % 4
+    arrived(mirror, 0, top)
+    send(feature_copy(5, gathered.at[mirror, top], mirror, 0, x_up, top))
+    send(feature_copy(6, gathered.at[mirror, top], mirror, 0, x_down, top))
+    arrived(beyond_down, 0, top)
+    send(feature_copy(7, gathered.at[beyond_down, top], beyond_down, 0, x_up, top))
+    arrived(mirror, 1, bottom)
+    send(feature_copy(11, gathered.at[mirror, bottom], mirror, 1, x_up, bottom))
+    send(feature_copy(12, gathered.at[mirror, bottom], mirror, 1, x_down, bottom))
+    arrived(beyond_up, 1, bottom)
+    send(feature_copy(8, gathered.at[beyond_up, bottom], beyond_up, 1, x_down, bottom))
+    for slot in (x_far, beyond_far):
+        arrived(slot, 0, top)
+        arrived(slot, 1, bottom)
+    arrived(beyond_down, 1, bottom)
+    arrived(beyond_up, 0, top)
     for copy in sent:
         copy.wait_send()
 
@@ -484,13 +504,21 @@
         )
 
     last[0] = summed(0).astype(BF16)
-    final = sum_copy(8, last.at[0], last.at[1], mirror)
+    final = sum_copy(8, last.at[0, top], last.at[1, top], mirror)
+    aside = remote(last.at[0, bottom], relay.at[1], rs_send.at[9], relay_recv.at[1], **along_z(7))
+    onward = remote(
+        relay.at[1], last.at[1, bottom], rs_send.at[10], rs_recv.at[9], **along_z(5)
+    )
+    aside.start()
     final.start()
+    aside.wait_recv()
+    onward.start()
     kept = summed(1)
     final.wait_recv()
+    onward.wait_recv()
     out[...] = (kept + last[1].astype(F32)).astype(BF16)
 
-    for copy in first_ups + first_downs + [c for pair in seconds for c in pair] + [final]:
+    for copy in first_ups + first_downs + [c for pair in seconds for c in pair] + [final, aside, onward]:
         copy.wait_send()
 
     @pl.when(ctx > 0)
@@ -570,8 +598,10 @@
             pltpu.VMEM((2, ROWS, 256), BF16),
             pltpu.VMEM((2, 2, ROWS, 256), BF16),
             pltpu.VMEM((2, ROWS, 256), BF16),
+            pltpu.VMEM((2, 128, 256), BF16),
+            dma((2,)),
             dma((6,)),
-            dma((9,)),
+            dma((13,)),
             dma((8, 2)),
             dma((3, 16)),
             dma((16,)),
@@ -579,8 +609,8 @@
             dma((2,)),
             dma((11,)),
             dma((11,)),
-            dma((9,)),
-            dma((9,)),
+            dma((11,)),
+            dma((10,)),
         ],
         compiler_params=pltpu.CompilerParams(
             collective_id=0, has_side_effects=True, vmem_limit_bytes=62 * 1024 * 1024

time: 94 us -> 99.7 us (1.061)
  the two profiles are of different devices: /device:TPU:112 before, /device:TPU:106 now
where the time goes in v4:
time: 99.7 us; the launch traced here: 99.5 us
  Pallas kernels  94.6 us (95%)
  local copies, waits for them, and re-layouts  4.25 us (4%)
    pallas_call x1, Pallas kernels, per_device(): pl.pallas_call(kernel, out_shape=(jax.ShapeDtypeStruct((ROWS, 256), BF16)...  94.6 us
    reshape x1, local copies, waits for them, and re-layouts, per_device(): return (attn_out, cache.reshape(5, PAGE, 2, 256))  2.68 us

profile of v4, /device:TPU:106, one launch (start us, length us, event | category | flops | bytes accessed | tf_op | source)
XLA Modules:
  0.0 99.5 jit_solution(9125849747306959315)
XLA Ops:
  0.6 94.6 %shard_map.95 = (bf16[256,256]{1,0:T(8,128)(2,1)}, bf16[5,128,512]{2,1,0:T(8,128)(2,1)}) custom-call(s32[3]{0:T(128)} %lengths.1, s32[3,64]{1,0:T(4,128)} %pages.1, bf16[256,256]{1,0:T(8,128)(2,1)} %hidden_h.1, f32[1,2048]{1,0:T(1,128)} %bitcast.2, f32[1,2048]{1,0:T(1,128)} %bitcast.3, f32[1,128]{1,0:T(1,128)} %constant.2.clone.inverse_h, ...), custom_call_target="tpu_custom_call" | custom-call | tf_op jit(solution)/shard_map/pallas_call | solution.py:569
  95.3 2.7 %reshape.15 = bf16[5,128,2,256]{3,2,1,0:T(2,128)(2,1)} reshape(bf16[5,128,512]{2,1,0:T(8,128)(2,1)} %get-tuple-element.5) | data formatting | bytes 1310720 | tf_op jit(solution)/shard_map/reshape | solution.py:622
  98.0 1.6 %copy.11 = bf16[256,256]{1,0:T(8,128)(2,1)} copy(bf16[256,256]{1,0:T(8,128)(2,1)} %get-tuple-element.8) | data formatting | bytes 262144

commit v5 on v4

--- a/solution.py
+++ b/solution.py
@@ -38,7 +38,7 @@
     out, cache,
     hidden, gain, bias, inverse, cosine, sine, gathered, normed, w_qkv_v, w_out_v, queries, pairs, every, best, total, acc,
     reply, weight, attended, terms, first, second, last,
-    relay, relay_recv, local_sem, ag_send, ag_recv, kv_send, kv_recv, far_send, far_recv, extra_send, extra_recv, rs_send, rs_recv,
+    local_sem, ag_send, ag_recv, kv_send, kv_recv, far_send, far_recv, extra_send, extra_recv, rs_send, rs_recv,
 ):
     ctx = lax.axis_index("ctx")
     tp = lax.axis_index("tp")
@@ -62,11 +62,6 @@
     is_helper = (ctx == 0) | (ctx == 16)
     is_helped = ctx == 32
 
-    def along_z(steps):
-        there = (half * 4 + ctx // 16 + steps) % 8
-        return {"ctx": (there % 4) * 16 + ctx % 16, "tp": (there // 4) * 4 + x}
-
-
     copies_in = [
         pltpu.make_async_copy(source, target, local_sem.at[number])
         for number, (source, target) in enumerate((
@@ -83,9 +78,6 @@
     for peer in (x_up, x_down, mirror):
         pl.semaphore_signal(barrier, inc=1, device_id={"tp": peer}, device_id_type=MESH)
 
-    for steps in (1, 3, 5, 7):
-        pl.semaphore_signal(barrier, inc=1, device_id=along_z(steps), device_id_type=MESH)
-
     @pl.when(ctx > 0)
     def _():
         pl.semaphore_signal(barrier, inc=1, device_id={"ctx": ctx - 1}, device_id_type=MESH)
@@ -105,7 +97,7 @@
 
     pl.semaphore_wait(
         barrier,
-        11 + jnp.where(ctx > 0, 1, 0) + jnp.where(ctx < 63, 1, 0)
+        7 + jnp.where(ctx > 0, 1, 0) + jnp.where(ctx < 63, 1, 0)
         + jnp.where(is_helper, 1, 0) + jnp.where(is_helped, 2, 0),
     )
 
@@ -117,13 +109,13 @@
 
     copies_in[0].wait()
     own_z = feature_copy(0, hidden.at[top], tp, 0, mirror, top)
-    own_relay = remote(hidden.at[bottom], relay.at[0], ag_send.at[9], relay_recv.at[0], **along_z(7))
+    own_rest = feature_copy(9, hidden.at[bottom], tp, 1, mirror, bottom)
     own_up = feature_copy(1, hidden, tp, 0, x_up)
     own_down = feature_copy(2, hidden, tp, 0, x_down)
-    for copy in (own_z, own_relay, own_up, own_down):
+    for copy in (own_z, own_rest, own_up, own_down):
         copy.start()
     gathered[tp] = hidden[...]
-    sent = [own_z, own_relay, own_up, own_down]
+    sent = [own_z, own_rest, own_up, own_down]
 
     copies_in[1].wait()
     index = ctx * ROWS + lax.broadcasted_iota(jnp.int32, (ROWS, 128), 0)
@@ -147,13 +139,6 @@
     def send(copy):
         copy.start()
         sent.append(copy)
-
-    own_relay.wait_recv()
-    origin = along_z(1)["tp"]
-    send(remote(
-        relay.at[0], gathered.at[origin, bottom], ag_send.at[10], ag_recv.at[origin, 1],
-        **along_z(5),
-    ))
 
     arrived(x_down, 0)
     send(feature_copy(3, gathered.at[x_down, top], x_down, 0, x_up, top))
@@ -504,21 +489,13 @@
         )
 
     last[0] = summed(0).astype(BF16)
-    final = sum_copy(8, last.at[0, top], last.at[1, top], mirror)
-    aside = remote(last.at[0, bottom], relay.at[1], rs_send.at[9], relay_recv.at[1], **along_z(7))
-    onward = remote(
-        relay.at[1], last.at[1, bottom], rs_send.at[10], rs_recv.at[9], **along_z(5)
-    )
-    aside.start()
+    final = sum_copy(8, last.at[0], last.at[1], mirror)
     final.start()
-    aside.wait_recv()
-    onward.start()
     kept = summed(1)
     final.wait_recv()
-    onward.wait_recv()
     out[...] = (kept + last[1].astype(F32)).astype(BF16)
 
-    for copy in first_ups + first_downs + [c for pair in seconds for c in pair] + [final, aside, onward]:
+    for copy in first_ups + first_downs + [c for pair in seconds for c in pair] + [final]:
         copy.wait_send()
 
     @pl.when(ctx > 0)
@@ -598,8 +575,6 @@
             pltpu.VMEM((2, ROWS, 256), BF16),
             pltpu.VMEM((2, 2, ROWS, 256), BF16),
             pltpu.VMEM((2, ROWS, 256), BF16),
-            pltpu.VMEM((2, 128, 256), BF16),
-            dma((2,)),
             dma((6,)),
             dma((13,)),
             dma((8, 2)),
@@ -609,8 +584,8 @@
             dma((2,)),
             dma((11,)),
             dma((11,)),
-            dma((11,)),
-            dma((10,)),
+            dma((9,)),
+            dma((9,)),
         ],
         compiler_params=pltpu.CompilerParams(
             collective_id=0, has_side_effects=True, vmem_limit_bytes=62 * 1024 * 1024

time: 99.7 us -> 95.1 us (0.954)
  the two profiles are of different devices: /device:TPU:106 before, /device:TPU:112 now
where the time goes in v5:
time: 95.1 us; the launch traced here: 95 us
  Pallas kernels  90.1 us (95%)
  local copies, waits for them, and re-layouts  4.25 us (4%)
    pallas_call x1, Pallas kernels, per_device(): pl.pallas_call(kernel, out_shape=(jax.ShapeDtypeStruct((ROWS, 256), BF16)...  90.1 us
    reshape x1, local copies, waits for them, and re-layouts, per_device(): return (attn_out, cache.reshape(5, PAGE, 2, 256))  2.68 us

profile of v5, /device:TPU:112, one launch (start us, length us, event | category | flops | bytes accessed | tf_op | source)
XLA Modules:
  0.0 95.0 jit_solution(15020484723366066692)
XLA Ops:
  0.6 90.1 %shard_map.95 = (bf16[256,256]{1,0:T(8,128)(2,1)}, bf16[5,128,512]{2,1,0:T(8,128)(2,1)}) custom-call(s32[3]{0:T(128)} %lengths.1, s32[3,64]{1,0:T(4,128)} %pages.1, bf16[256,256]{1,0:T(8,128)(2,1)} %hidden_h.1, f32[1,2048]{1,0:T(1,128)} %bitcast.2, f32[1,2048]{1,0:T(1,128)} %bitcast.3, f32[1,128]{1,0:T(1,128)} %constant.2.clone.inverse_h, ...), custom_call_target="tpu_custom_call" | custom-call | tf_op jit(solution)/shard_map/pallas_call | solution.py:546
  90.7 2.7 %reshape.15 = bf16[5,128,2,256]{3,2,1,0:T(2,128)(2,1)} reshape(bf16[5,128,512]{2,1,0:T(8,128)(2,1)} %get-tuple-element.5) | data formatting | bytes 1310720 | tf_op jit(solution)/shard_map/reshape | solution.py:597
  93.4 1.6 %copy.11 = bf16[256,256]{1,0:T(8,128)(2,1)} copy(bf16[256,256]{1,0:T(8,128)(2,1)} %get-tuple-element.8) | data formatting | bytes 262144
